TPU v7x, 256 devices: a whole 4x4x8 slice. The times are simulated.
256 devices in a mesh: owner: 16 (over z, core), tensor: 16 (over x, y).
Axes of the slice: x: 4, y: 4, z: 8, core: 2. Of those that a mesh axis runs over, the one named last changes fastest.
Arguments:
- mixer_input: bfloat16 [16384, 2, 8192], P('owner', None, 'tensor'), may hold values from -6 to 6
- step_raw: float32 [16384, 128], P('owner', 'tensor'), may hold values from -7 to 5
- decay_rate: float32 [128], P('tensor'), may hold values from 0.005 to 0.5
- skip_gain: float32 [128], P('tensor'), may hold values from 0.5 to 2
- state_proj: bfloat16 [16384, 2, 4, 256], P('owner'), may hold values from -1.5 to 1.5
- queries: bfloat16 [16384, 4096], P('owner', 'tensor'), may hold values from -256 to 256
- suffix_kv: bfloat16 [16384, 2, 4, 128], P('owner'), may hold values from -6 to 6
- state_pool: bfloat16 [64, 128, 64, 256], P('owner', 'tensor'), may hold values from -1.5 to 1.5
- page_pool: bfloat16 [256, 128, 2, 4, 128], P('owner'), may hold values from -6 to 6
- norm_gain: float32 [8192], P('tensor'), may hold values from 0.1 to 1.9
- hit_owner: int32 [64, 1], replicated, may hold values from 0 to 15; in each aligned block of 4 rows (0 to 3, 4 to 7, ...) at most 2 rows name the same one
- hit_slot: int32 [64], replicated, may hold values from 0 to 3
- page_owner: int32 [64, 16, 1], replicated, may hold values from 0 to 15; in each aligned block of 64 rows (0 to 63, 64 to 127, ..., all dimensions but the last counted through in order) at most 6 rows name the same one
- page_slot: int32 [64, 16], replicated, may hold values from 0 to 15
- prefix_len: int32 [64], replicated, may hold values from 256 to 2048, as said below
- suffix_len: int32 [64], replicated, may hold values from 64 to 256, as said below
Outputs:
- mamba_out: bfloat16 [16384, 8192], P('owner', 'tensor')
- attn_out: bfloat16 [16384, 4096], P('owner', 'tensor')
Inputs may be any that keep to these rules, and one draw needn't show every extreme that they name: `hit_owner`: the 4 requests on one index of owner name one owner at most 2 times, and some index reaches it. `page_owner`: of the 64 list entries of the requests on one index of owner, at most 6 name one owner, and some index reaches it. `prefix_len`: a multiple of 256; request 0 has 2048. `suffix_len`: request 0 has 256.
All inputs are finite; a program needn't handle non-finite values.
Results may differ from a plain program's by a relative error of at most 0.0045.
Values may be sent and summed in bfloat16 or wider, within the bound.
A program may use at most 192 MiB of HBM per device.

v0:
```python
import math

import jax
import jax.numpy as jnp
from jax import lax
from jax.sharding import PartitionSpec as P

SSM_HEAD_TOTAL = 128
MHDIM = 64
STATE = 256
GROUPS = 4
QHEADS = 32
KVHEADS = 4
HD = 128
PAGE = 128
SPAN = 128
SUF = 256
CAP_S = 2
MAXP = 16


EPSILON = 1e-05
NEG_FILL = -1e30


def mixer_core(x_heads, z_heads, rate_raw, decay_groups, skip_groups, b_rows, c_rows, start_state):
    seq_len, group_count, head_count, head_width = x_heads.shape
    blocks = seq_len // SPAN
    step_rate = jax.nn.softplus(rate_raw)
    keep_log = -step_rate * decay_groups[None]
    x_block = x_heads.reshape(blocks, SPAN, group_count, head_count, head_width)
    rate_block = step_rate.reshape(blocks, SPAN, group_count, head_count)
    cum_block = jnp.cumsum(keep_log.reshape(blocks, SPAN, group_count, head_count), axis=1)
    b_block = b_rows.reshape(blocks, SPAN, group_count, -1)
    c_block = c_rows.reshape(blocks, SPAN, group_count, -1)
    intersection = jnp.einsum(
        "cign,cjgn->cgij", c_block, b_block, preferred_element_type=jnp.float32
    )
    cum_moved = jnp.transpose(cum_block, (0, 2, 3, 1))
    rate_moved = jnp.transpose(rate_block, (0, 2, 3, 1))
    lower = jnp.arange(SPAN)[:, None] >= jnp.arange(SPAN)[None, :]
    fade = jnp.exp(jnp.where(lower, cum_moved[..., :, None] - cum_moved[..., None, :], NEG_FILL))
    weights = (intersection[:, :, None] * fade * rate_moved[..., None, :]).astype(jnp.bfloat16)
    inner = jnp.einsum("cghij,cjghp->cighp", weights, x_block, preferred_element_type=jnp.float32)
    cum_end = cum_block[:, -1]
    tail = jnp.exp(cum_end[:, None] - cum_block) * rate_block
    scaled = (tail[..., None] * x_block).astype(jnp.bfloat16)
    block_state = jnp.einsum(
        "cjghp,cjgn->cghpn", scaled, b_block, preferred_element_type=jnp.float32
    )
    carry = start_state.astype(jnp.float32)
    begins = []
    for block_index in range(blocks):
        begins.append(carry)
        carry = jnp.exp(cum_end[block_index])[..., None, None] * carry + block_state[block_index]
    begin_half = jnp.stack(begins).astype(jnp.bfloat16)
    carried = jnp.einsum(
        "cign,cghpn->cighp", c_block, begin_half, preferred_element_type=jnp.float32
    )
    summed = (
        inner
        + jnp.exp(cum_block)[..., None] * carried
        + skip_groups[None, None, :, :, None] * x_block
    )
    gate = jax.nn.silu(z_heads.astype(jnp.float32)).reshape(
        blocks, SPAN, group_count, head_count, head_width
    )
    return (summed * gate).reshape(seq_len, group_count, head_count, head_width)


def attend(query, key_pre, value_pre, key_suf, value_suf, prefix_count):
    softmax_scale = 1.0 / math.sqrt(HD)
    score_pre = (
        jnp.einsum("qhd,md->hqm", query, key_pre, preferred_element_type=jnp.float32)
        * softmax_scale
    )
    score_suf = (
        jnp.einsum("qhd,kd->hqk", query, key_suf, preferred_element_type=jnp.float32)
        * softmax_scale
    )
    pre_live = jnp.arange(key_pre.shape[0]) < prefix_count
    causal = jnp.arange(SUF)[:, None] >= jnp.arange(SUF)[None, :]
    score_pre = jnp.where(pre_live[None, None, :], score_pre, NEG_FILL)
    score_suf = jnp.where(causal[None], score_suf, NEG_FILL)
    row_max = jnp.maximum(jnp.max(score_pre, axis=2), jnp.max(score_suf, axis=2))
    weight_pre = jnp.exp(score_pre - row_max[..., None])
    weight_suf = jnp.exp(score_suf - row_max[..., None])
    denominator = jnp.sum(weight_pre, axis=2) + jnp.sum(weight_suf, axis=2)
    mixed = jnp.einsum(
        "hqm,md->qhd",
        weight_pre.astype(jnp.bfloat16),
        value_pre,
        preferred_element_type=jnp.float32,
    )
    mixed = mixed + jnp.einsum(
        "hqk,kd->qhd",
        weight_suf.astype(jnp.bfloat16),
        value_suf,
        preferred_element_type=jnp.float32,
    )
    return mixed / jnp.transpose(denominator)[:, :, None]


def bucket_plan(owner_rows, live_rows, owner_index, capacity):
    positions = jnp.arange(owner_rows.shape[1])
    matches = (
        (owner_rows[:, :, None] == owner_rows[:, None, :])
        & live_rows[:, None, :]
        & (positions[None, None, :] < positions[None, :, None])
    )
    slot_rank = jnp.sum(matches.astype(jnp.int32), axis=2)
    chosen = (
        (owner_rows[:, None, :] == owner_index)
        & live_rows[:, None, :]
        & (slot_rank[:, None, :] == jnp.arange(capacity)[None, :, None])
    )
    return (slot_rank, chosen)


def bucket_send(table, entry_ids, chosen):
    wanted = jnp.sum(jnp.where(chosen, entry_ids[:, None, :], 0), axis=2).reshape(-1)
    filled = jnp.any(chosen, axis=2).reshape(-1)
    picked = jnp.take(table, wanted, axis=0, mode="clip")
    shaped = jnp.where(
        filled.reshape((-1,) + (1,) * (picked.ndim - 1)), picked, jnp.zeros_like(picked)
    )
    return shaped.reshape(chosen.shape[:2] + picked.shape[1:])


def body(
    mixer_input,
    step_raw,
    decay_rate,
    skip_gain,
    state_proj,
    queries,
    suffix_kv,
    state_pool,
    page_pool,
    norm_gain,
    hit_owner,
    hit_slot,
    page_owner,
    page_slot,
    prefix_len,
    suffix_len,
):
    owners = lax.axis_size("owner")
    owner_index = lax.axis_index("owner")
    column = lax.axis_index("tensor")
    local_count = mixer_input.shape[0] // SUF
    local_heads = decay_rate.shape[0]
    local_qheads = queries.shape[1] // HD
    group_index = column * local_heads // (SSM_HEAD_TOTAL // GROUPS)
    kv_index = column * local_qheads // (QHEADS // KVHEADS)
    first_row = owner_index * local_count
    page_capacity = max(2, (local_count * MAXP + owners - 1) // owners * 3 // 2)
    state_owner = hit_owner[:, 0].reshape(owners, local_count)
    state_slot = hit_slot.reshape(owners, local_count)
    every_live = jnp.ones(state_owner.shape, jnp.bool_)
    state_rank, state_pick = bucket_plan(state_owner, every_live, owner_index, CAP_S)
    outgoing = bucket_send(state_pool, state_slot, state_pick)
    arrived = lax.all_to_all(outgoing, "owner", split_axis=0, concat_axis=0, tiled=True)
    arrived = arrived.reshape((owners * CAP_S,) + arrived.shape[2:])
    local_holder = lax.dynamic_index_in_dim(state_owner, owner_index, 0, keepdims=False)
    my_rank = lax.dynamic_index_in_dim(state_rank, owner_index, 0, keepdims=False)
    start_state = jnp.take(arrived, local_holder * CAP_S + my_rank, axis=0, mode="clip")
    x_heads = mixer_input[:, 0].reshape(local_count, SUF, 1, local_heads, MHDIM)
    z_heads = mixer_input[:, 1].reshape(local_count, SUF, 1, local_heads, MHDIM)
    rate_raw = step_raw.reshape(local_count, SUF, 1, local_heads)
    maps_here = lax.dynamic_index_in_dim(state_proj, group_index, 2, keepdims=True)
    b_rows = maps_here[:, 0].reshape(local_count, SUF, 1, STATE)
    c_rows = maps_here[:, 1].reshape(local_count, SUF, 1, STATE)
    core = jax.vmap(mixer_core, in_axes=(0, 0, 0, None, None, 0, 0, 0))
    gated = core(
        x_heads,
        z_heads,
        rate_raw,
        decay_rate.reshape(1, local_heads),
        skip_gain.reshape(1, local_heads),
        b_rows,
        c_rows,
        start_state.reshape(local_count, 1, local_heads, MHDIM, STATE),
    )
    gated = gated.reshape(local_count * SUF, local_heads * MHDIM)
    partial_sum = jnp.sum(gated * gated, axis=1)
    spread = jnp.where(jnp.arange(GROUPS)[:, None] == group_index, partial_sum[None, :], 0.0)
    totals = lax.psum(spread, "tensor")
    square = lax.dynamic_index_in_dim(totals, group_index, 0, keepdims=False) / (
        SSM_HEAD_TOTAL // GROUPS * MHDIM
    )
    my_suffix = lax.dynamic_slice_in_dim(suffix_len, first_row, local_count, 0)
    active = (jnp.arange(SUF)[None, :] < my_suffix[:, None]).reshape(-1)
    rescaled_input = gated * lax.rsqrt(square + EPSILON)[:, None] * norm_gain[None, :]
    mamba_out = jnp.where(active[:, None], rescaled_input, 0.0).astype(jnp.bfloat16)
    pool_head = lax.dynamic_index_in_dim(page_pool, kv_index, 3, keepdims=False)
    entries = local_count * MAXP
    page_rows = page_owner[:, :, 0].reshape(owners, entries)
    page_ids = page_slot.reshape(owners, entries)
    live_rows = (jnp.arange(MAXP)[None, :] * PAGE < prefix_len[:, None]).reshape(owners, entries)
    my_pages = lax.dynamic_index_in_dim(page_rows, owner_index, 0, keepdims=False)
    my_live = lax.dynamic_index_in_dim(live_rows, owner_index, 0, keepdims=False)
    page_rank, page_pick = bucket_plan(page_rows, live_rows, owner_index, page_capacity)
    sending = bucket_send(pool_head, page_ids, page_pick)
    received_rows = lax.all_to_all(sending, "owner", split_axis=0, concat_axis=0, tiled=True)
    received_rows = received_rows.reshape((owners * page_capacity,) + received_rows.shape[2:])
    my_page_rank = lax.dynamic_index_in_dim(page_rank, owner_index, 0, keepdims=False)
    fetched = jnp.take(received_rows, my_pages * page_capacity + my_page_rank, axis=0, mode="clip")
    fetched = jnp.where(my_live[:, None, None, None], fetched, jnp.zeros_like(fetched))
    prefix_kv = fetched.reshape(local_count, MAXP * PAGE, 2, HD)
    my_prefix = lax.dynamic_slice_in_dim(prefix_len, first_row, local_count, 0)
    owned_key_value = lax.dynamic_index_in_dim(suffix_kv, kv_index, 2, keepdims=False).reshape(
        local_count, SUF, 2, HD
    )
    query = queries.reshape(local_count, SUF, local_qheads, HD)
    mixed = jax.vmap(attend)(
        query,
        prefix_kv[:, :, 0],
        prefix_kv[:, :, 1],
        owned_key_value[:, :, 0],
        owned_key_value[:, :, 1],
        my_prefix,
    )
    attn_rows = mixed.reshape(local_count * SUF, local_qheads * HD)
    attn_out = jnp.where(active[:, None], attn_rows, 0.0).astype(jnp.bfloat16)
    return (mamba_out, attn_out)


def solution(mesh):
    return jax.shard_map(
        body,
        mesh=mesh,
        in_specs=(
            P("owner", None, "tensor"),
            P("owner", "tensor"),
            P("tensor"),
            P("tensor"),
            P("owner", None, None, None),
            P("owner", "tensor"),
            P("owner", None, None, None),
            P("owner", "tensor", None, None),
            P("owner", None, None, None, None),
            P("tensor"),
            P(),
            P(),
            P(),
            P(),
            P(),
            P(),
        ),
        out_specs=(P("owner", "tensor"), P("owner", "tensor")),
        check_vma=False,
    )
```

profile of v0, /device:TPU:6, one launch (start us, length us, event | category | flops | bytes accessed | tf_op | source)
XLA Modules:
  0.0 442.8 jit_solution(13598574537655978479)
XLA Ops:
  0.7 0.9 copy.186
  1.7 0.7 lt.143
  2.7 4.6 %constant_dynamic-slice_fusion.4 = bf16[16,128,2,1,128]{4,3,2,1,0:T(2,128)(2,1)S(1)} fusion(bf16[16,128,2,4,128]{4,3,2,1,0:T(4,128)(2,1)} %param.24, s32[]{:T(128)S(6)} %select_n.125), kind=kLoop, calls=%fused_computation.95 | loop fusion | bytes 2097156 | tf_op jit(solution)/shard_map/jit(dynamic_index_in_dim)/dynamic_slice | solution.py:196
  7.3 0.3 copy.249
  7.6 0.4 copy-done.11
  8.2 0.5 convert_reduce_fusion
  8.7 0.2 fusion.36
  8.9 0.2 select_reduce_fusion
  9.3 0.1 copy.187
  9.4 5.9 %gather_fusion.2 = bf16[96,128,2,128]{3,1,2,0:T(8,128)(2,1)} fusion(bf16[16,128,2,128]{3,1,2,0:T(8,128)(2,1)S(1)} %bitcast.137, s32[1024]{0:T(1024)S(1)} %pad_clamp_fusion.1), kind=kCustom, calls=%fused_computation.2 | custom fusion | bytes 12583296 | tf_op jit(solution)/shard_map/jit(_take)/gather | solution.py:123
  15.3 5.9 %broadcast_select_fusion.1 = bf16[16,6,128,2,128]{4,2,3,1,0:T(8,128)(2,1)} fusion(bf16[16,6,128,2,128]{4,2,3,1,0:T(8,128)(2,1)} %bitcast.139, pred[16,6]{1,0:T(8,128)(4,1)S(1)} %copy.187), kind=kLoop, calls=%fused_computation.13 | loop fusion | flops 3145728 | bytes 12583008 | tf_op jit(solution)/shard_map/jit(_where)/select_n | solution.py:124
  21.3 8.7 %all-to-all-start.1 = ((bf16[16,6,128,2,128]{4,2,3,1,0:T(8,128)(2,1)}), bf16[16,6,128,2,128]{4,2,3,1,0:T(8,128)(2,1)}, u32[]{:S(2)}, u32[]{:S(2)}) async-start(bf16[16,6,128,2,128]{4,2,3,1,0:T(8,128)(2,1)} %broadcast_select_fusion.1), calls=%async_computation.1 | async-start | bytes 12582912 | tf_op jit(solution)/shard_map/all_to_all | solution.py:205
  30.2 0.5 broadcast.269
  30.7 0.7 reduce.10
  31.6 0.1 copy.168
  32.0 0.1 copy.171
  32.1 4.7 %gather_fusion = bf16[32,8,64,256]{3,2,1,0:T(8,128)(2,1)} fusion(bf16[4,8,64,256]{3,2,1,0:T(8,128)(2,1)S(1)} %copy-done.2, s32[1024]{0:T(1024)S(1)} %pad_clamp_fusion.3), kind=kCustom, calls=%fused_computation | custom fusion | bytes 16777344 | tf_op jit(solution)/shard_map/jit(_take)/gather | solution.py:123
  36.8 7.2 %broadcast_select_fusion = bf16[16,2,8,64,256]{4,3,2,1,0:T(8,128)(2,1)} fusion(bf16[16,2,8,64,256]{4,3,2,1,0:T(8,128)(2,1)} %bitcast.138, pred[16,2]{1,0:T(8,128)(4,1)S(1)} %copy.171), kind=kLoop, calls=%fused_computation.12 | loop fusion | flops 4194304 | bytes 16777248 | tf_op jit(solution)/shard_map/jit(_where)/select_n | solution.py:124
  44.0 125.2 %all-to-all-done.1 = bf16[16,6,128,2,128]{4,2,3,1,0:T(8,128)(2,1)} async-done(((bf16[16,6,128,2,128]{4,2,3,1,0:T(8,128)(2,1)}), bf16[16,6,128,2,128]{4,2,3,1,0:T(8,128)(2,1)}, u32[]{:S(2)}, u32[]{:S(2)}) %all-to-all-start.1) | async-done | bytes 6291488 | tf_op jit(solution)/shard_map/all_to_all | solution.py:205
  169.3 5.0 %all-to-all-start = ((bf16[16,2,8,64,256]{4,3,2,1,0:T(8,128)(2,1)}), bf16[16,2,8,64,256]{4,3,2,1,0:T(8,128)(2,1)}, u32[]{:S(2)}, u32[]{:S(2)}) async-start(bf16[16,2,8,64,256]{4,3,2,1,0:T(8,128)(2,1)} %broadcast_select_fusion), calls=%async_computation | async-start | bytes 16777216 | tf_op jit(solution)/shard_map/all_to_all | solution.py:163
  174.3 6.9 %fusion.50 = (bf16[1024,1,512]{2,1,0:T(2,128)(2,1)}, bf16[1024,1,512]{2,1,0:T(2,128)(2,1)}) fusion(bf16[1024,2,512]{2,1,0:T(2,128)(2,1)} %param.16), kind=kLoop, calls=%fused_computation.115 | loop fusion | bytes 4194304 | tf_op jit(solution)/shard_map/slice | solution.py:169
  181.2 5.8 %copy.165 = bf16[1024,1,512]{0,2,1:T(8,128)(2,1)} copy(bf16[1024,1,512]{2,1,0:T(2,128)(2,1)} %get-tuple-element.15) | data formatting | bytes 2097152 | tf_op jit(solution)/shard_map/slice | solution.py:168
  187.1 4.7 %copy_convert_fusion = (f32[1024,1,512]{2,0,1:T(8,128)}, f32[1024,1,512]{2,0,1:T(8,128)}) fusion(bf16[1024,1,512]{2,1,0:T(2,128)(2,1)} %get-tuple-element.14, bf16[1024,1,512]{2,1,0:T(2,128)(2,1)} %get-tuple-element.15), kind=kLoop, calls=%fused_computation.52 | loop fusion | flops 1048576 | bytes 6291456 | tf_op jit(solution)/shard_map/vmap()/convert_element_type | solution.py:65
  191.8 6.1 %copy.182 = f32[1024,1,512]{0,1,2:T(1,128)} copy(f32[1024,1,512]{2,0,1:T(8,128)} %get-tuple-element.26) | data formatting | bytes 4194304 | tf_op jit(solution)/shard_map/vmap()/convert_element_type | solution.py:65
  198.0 6.1 %copy.179 = f32[1024,1,512]{0,1,2:T(1,128)} copy(f32[1024,1,512]{2,0,1:T(8,128)} %get-tuple-element.27) | data formatting | bytes 4194304 | tf_op jit(solution)/shard_map/vmap()/convert_element_type | solution.py:47
  204.1 5.4 %constant_dynamic-slice_fusion.8 = (bf16[1024,1,1,256]{3,2,1,0:T(2,128)(2,1)}, bf16[1024,1,1,256]{3,2,1,0:T(2,128)(2,1)S(1)}) fusion(bf16[1024,2,4,256]{3,2,1,0:T(4,128)(2,1)} %param.20, s32[]{:T(128)S(6)} %select_n.115, s32[]{:T(128)S(6)} %add.163), kind=kLoop, calls=%fused_computation.99 | loop fusion | bytes 2097160 | tf_op jit(solution)/shard_map/slice | solution.py:172
  209.5 1.0 copy.175
  210.6 1.0 copy.161
  211.6 1.4 fusion.53
  213.0 2.4 fusion.51
  215.4 1.2 copy.167
  216.6 0.2 copy.162
  216.8 1.3 copy.215
  218.2 2.6 reshape.579
  220.7 1.2 copy.176
  222.2 2.0 reshape.584
  224.4 1.1 constant_dynamic-slice_fusion.1
  225.6 0.2 fusion.42
  225.9 0.8 multiply_convert_fusion.2
  226.7 2.7 convolution_bitcast_fusion
  229.5 0.3 fusion.54
  229.8 0.5 fusion.52
  230.3 3.3 fusion.6
  233.7 5.9 %gather_fusion.3 = bf16[64,128,2,128]{3,1,2,0:T(8,128)(2,1)} fusion(bf16[96,128,2,128]{3,1,2,0:T(8,128)(2,1)} %bitcast.33, s32[1024]{0:T(1024)S(1)} %pad_clamp_fusion), kind=kCustom, calls=%fused_computation.3 | custom fusion | bytes 8388864 | tf_op jit(solution)/shard_map/jit(_take)/gather | solution.py:208
  239.6 2.5 copy.191
  242.1 2.1 bitcast_select_fusion
  244.3 3.2 bitcast_reduce_fusion
  247.5 0.3 fusion.21
  247.8 4.5 %fusion.1 = f32[4,2,256]{2,1,0:T(2,128)S(1)} fusion(f32[4,2048,256,2]{2,1,3,0:T(8,128)S(1)} %get-tuple-element.23, f32[4,2,256]{2,1,0:T(2,128)S(1)} %max.43, pred[4,2048]{1,0:T(4,128)(4,1)S(1)} %iota_compare_fusion.3), kind=kLoop, calls=%fused_computation.8 | loop fusion | flops 16775168 | bytes 16801792 | tf_op jit(solution)/shard_map/vmap()/reduce_sum | solution.py:88
  252.3 4.7 %fusion.3 = f32[4,128,2,256]{3,1,2,0:T(8,128)S(1)} fusion(f32[4,2048,256,2]{2,1,3,0:T(8,128)S(1)} %get-tuple-element.23, f32[4,2,256]{2,1,0:T(2,128)S(1)} %max.43, pred[4,2048]{1,0:T(4,128)(4,1)S(1)} %iota_compare_fusion.3, bf16[4,2048,2,128]{3,1,0,2:T(8,128)(2,1)S(1)} %bitcast_select_fusion), kind=kOutput, calls=%fused_computation.10 | convolution fusion | flops 1090519040 | bytes 19939328 | tf_op jit(solution)/shard_map/vmap(hqm,md->qhd)/dot_general | solution.py:89
  257.1 1.3 fusion.26
  258.4 1.3 copy.199
  259.7 1.0 fusion.28
  260.7 97.6 %all-to-all-done = bf16[16,2,8,64,256]{4,3,2,1,0:T(8,128)(2,1)} async-done(((bf16[16,2,8,64,256]{4,3,2,1,0:T(8,128)(2,1)}), bf16[16,2,8,64,256]{4,3,2,1,0:T(8,128)(2,1)}, u32[]{:S(2)}, u32[]{:S(2)}) %all-to-all-start) | async-done | bytes 8388640 | tf_op jit(solution)/shard_map/all_to_all | solution.py:163
  358.3 4.0 gather_fusion.1
  362.3 2.0 fusion.9
  364.4 0.1 copy-done.4
  364.5 0.6 copy-done.5
  365.1 2.6 multiply_reduce_fusion
  367.7 1.6 copy.185
  369.4 2.7 reshape.582
  372.2 67.3 %psum.7 = f32[4,1024]{1,0:T(4,128)S(1)} all-reduce(f32[4,1024]{1,0:T(4,128)S(1)} %broadcast_select_fusion.2), channel_id=1, replica_groups=mesh['owner'=16,'tensor'=16] {'tensor'}, use_global_device_ids=true, to_apply=%region_5.6 | all-reduce | flops 4096 | bytes 32768 | tf_op jit(solution)/shard_map/psum | solution.py:188
  439.5 2.0 select_convert_fusion
  441.5 1.3 copy.200
  (84 shorter events, 2.4 us)
Async XLA Ops:
  0.6 223.8 %copy-start = (bf16[1024,2,4,128]{3,2,1,0:T(4,128)(2,1)S(1)}, bf16[1024,2,4,128]{3,2,1,0:T(4,128)(2,1)}, u32[]{:S(2)}) copy-start(bf16[1024,2,4,128]{3,2,1,0:T(4,128)(2,1)} %param.22) | copy-start | bytes 6291460
  7.3 0.7 copy-start.11
  21.3 8.8 %copy-start.14 = (s32[64]{0:T(128)S(1)}, s32[64]{0:T(128)}, u32[]{:S(2)}) copy-start(s32[64]{0:T(128)} %param.27) | copy-start | bytes 772
  21.3 9.5 %copy-start.16 = (s32[64,1]{0,1:T(1,128)S(1)}, s32[64,1]{0,1:T(1,128)}, u32[]{:S(2)}) copy-start(s32[64,1]{0,1:T(1,128)} %param.26) | copy-start | bytes 772
  21.3 10.8 %copy-start.2 = (bf16[4,8,64,256]{3,2,1,0:T(8,128)(2,1)S(1)}, bf16[4,8,64,256]{3,2,1,0:T(8,128)(2,1)}, u32[]{:S(2)}) copy-start(bf16[4,8,64,256]{3,2,1,0:T(8,128)(2,1)} %param.23) | copy-start | bytes 3145732
  21.3 148.0 %all-to-all-start.1 = ((bf16[16,6,128,2,128]{4,2,3,1,0:T(8,128)(2,1)}), bf16[16,6,128,2,128]{4,2,3,1,0:T(8,128)(2,1)}, u32[]{:S(2)}, u32[]{:S(2)}) async-start(bf16[16,6,128,2,128]{4,2,3,1,0:T(8,128)(2,1)} %broadcast_select_fusion.1), calls=%async_computation.1 | async-start | bytes 12582912 | tf_op jit(solution)/shard_map/all_to_all | solution.py:205
  169.3 189.0 %all-to-all-start = ((bf16[16,2,8,64,256]{4,3,2,1,0:T(8,128)(2,1)}), bf16[16,2,8,64,256]{4,3,2,1,0:T(8,128)(2,1)}, u32[]{:S(2)}, u32[]{:S(2)}) async-start(bf16[16,2,8,64,256]{4,3,2,1,0:T(8,128)(2,1)} %broadcast_select_fusion), calls=%async_computation | async-start | bytes 16777216 | tf_op jit(solution)/shard_map/all_to_all | solution.py:163
  204.1 5.5 %copy-start.10 = (f32[1024,8]{0,1:T(8,128)S(1)}, f32[1024,8]{0,1:T(8,128)}, u32[]{:S(2)}) copy-start(f32[1024,8]{0,1:T(8,128)} %param.17) | copy-start | bytes 98308
  209.4 1.1 copy-start.13
  216.8 5.1 %copy-start.15 = (s32[64]{0:T(128)S(1)}, s32[64]{0:T(128)}, u32[]{:S(2)}) copy-start(s32[64]{0:T(128)} %param.30) | copy-start | bytes 772
  216.8 5.2 %copy-start.17 = (s32[64]{0:T(128)S(1)}, s32[64]{0:T(128)}, u32[]{:S(2)}) copy-start(s32[64]{0:T(128)} %param.31) | copy-start | bytes 772
  224.3 1.6 copy-start.3
  225.6 4.2 copy-start.6
  226.7 3.1 copy-start.8
  242.1 2.1 copy-start.9
  252.3 4.8 %copy-start.7 = (bf16[1024,2,1,128]{3,0,1,2:T(8,128)(2,1)S(1)}, bf16[1024,2,1,128]{3,0,1,2:T(8,128)(2,1)}, u32[]{:S(2)}) copy-start(bf16[1024,2,1,128]{3,0,1,2:T(8,128)(2,1)} %copy-done.6) | copy-start | bytes 1572868
  362.3 2.2 copy-start.4
  362.3 2.8 copy-start.5
  362.3 2.8 copy-start.18
  369.3 70.1 %copy-start.12 = (f32[512]{0:T(512)S(1)}, f32[512]{0:T(512)}, u32[]{:S(2)}) copy-start(f32[512]{0:T(512)} %param.25) | copy-start | bytes 6148
  439.5 3.4 copy-start.1
where the time goes:
time: 450 us; the launch traced here: 443 us
  waiting for transfers between devices  223 us (50%)
  local copies, waits for them, and re-layouts  82.4 us (18%)
  blocking collectives  67.3 us (15%)
  other arithmetic  36.9 us (8%)
  matrix products  18.6 us (4%)
  starting transfers between devices  13.7 us (3%)
    all_to_all x1, waiting for transfers between devices, body(): lax.all_to_all(sending, 'owner', split_axis=0, concat_axis=0, tiled=True)  125 us
    all_to_all x1, waiting for transfers between devices, body(): lax.all_to_all(outgoing, 'owner', split_axis=0, concat_axis=0, tiled=True)  97.6 us
    psum x1, blocking collectives, body(): totals = lax.psum(spread, 'tensor')  67.3 us
    select_n x2, other arithmetic, bucket_send(): jnp.where(filled.reshape((-1,) + (1,) * (picked.ndim - 1)), picked, jnp.z...  13.1 us
    gather x2, local copies, waits for them, and re-layouts, bucket_send(): picked = jnp.take(table, wanted, axis=0, mode='clip')  10.6 us
  transfers between devices with their start and end apart: 2, of which 2 were waited for; matrix products, arithmetic and copies ran while one was open for 23% of the time, Pallas kernels for 0%

commit v1 on v0

v1 whole, which is shorter than its diff:
```python
import functools
import math

import jax
import jax.numpy as jnp
from jax import lax
from jax.experimental import pallas as pl
from jax.experimental.pallas import tpu as pltpu
from jax.sharding import Mesh
from jax.sharding import PartitionSpec as P

HEADS = 8
MHDIM = 64
CH = HEADS * MHDIM
STATE = 256
GROUP_CH = 2048
HD = 128
PAGE = 128
SPAN = 128
SUF = 256
MAXP = 16
REQ = 4
QUARTER = PAGE // 4
EPSILON = 1e-05
NEG = -1e30
OWN = ("z", "core")
BF = jnp.bfloat16
F32 = jnp.float32
HI = lax.Precision.HIGHEST


def dot_nt(a, b):
    return lax.dot_general(a, b, (((1,), (1,)), ((), ())), preferred_element_type=F32)


def dot_nn(a, b):
    return lax.dot_general(a, b, (((1,), (0,)), ((), ())), preferred_element_type=F32)


def dot_tn(a, b):
    return lax.dot_general(a, b, (((0,), (0,)), ((), ())), preferred_element_type=F32)


def expand(cols):
    head = lax.broadcasted_iota(jnp.int32, (HEADS, CH), 0)
    chan = lax.broadcasted_iota(jnp.int32, (HEADS, CH), 1)
    pick = (chan // MHDIM == head).astype(F32)
    return lax.dot_general(
        cols, pick, (((1,), (0,)), ((), ())), preferred_element_type=F32, precision=HI
    )


def mixer_local_kernel(x_ref, z_ref, step_ref, decay_ref, skip_ref, b_ref, c_ref, p_ref, e_ref, bs_ref, dec_ref):
    lane = lax.broadcasted_iota(jnp.int32, (HEADS, SPAN), 1)
    row = lax.broadcasted_iota(jnp.int32, (SPAN, SPAN), 0)
    col = lax.broadcasted_iota(jnp.int32, (SPAN, SPAN), 1)
    lower = row >= col
    low_half = lax.broadcasted_iota(jnp.int32, (SPAN, 2 * MHDIM), 1) < MHDIM
    for blk in range(SUF // SPAN):
        rows = pl.ds(blk * SPAN, SPAN)
        raw = step_ref[:, rows]
        rate = jnp.maximum(raw, 0.0) + jnp.log(1.0 + jnp.exp(-jnp.abs(raw)))
        cum = -rate * decay_ref[...]
        shift = 1
        while shift < SPAN:
            cum = cum + jnp.where(lane >= shift, pltpu.roll(cum, shift, 1), 0.0)
            shift *= 2
        cum_col = jnp.transpose(cum)
        x = x_ref[rows, :]
        b = b_ref[rows, :]
        c = c_ref[rows, :]
        inter = dot_nt(c, b)
        for pair in range(HEADS // 2):
            parts = []
            for h in (2 * pair, 2 * pair + 1):
                gap = cum_col[:, h : h + 1] - cum[h : h + 1, :]
                fade = jnp.exp(jnp.where(lower, gap, NEG))
                parts.append((inter * fade * rate[h : h + 1, :]).astype(BF))
            lanes = pl.ds(pair * 2 * MHDIM, 2 * MHDIM)
            xp = x_ref[rows, lanes]
            first = dot_nn(parts[0], xp)
            second = dot_nn(parts[1], xp)
            inner = jnp.where(low_half, first, second)
            z = z_ref[rows, lanes].astype(F32)
            gate = z / (1.0 + jnp.exp(-z))
            p_ref[rows, lanes] = (inner + skip_ref[:, lanes] * xp.astype(F32)) * gate
            grow = jnp.where(
                low_half,
                jnp.broadcast_to(cum_col[:, 2 * pair : 2 * pair + 1], (SPAN, 2 * MHDIM)),
                jnp.broadcast_to(cum_col[:, 2 * pair + 1 : 2 * pair + 2], (SPAN, 2 * MHDIM)),
            )
            e_ref[rows, lanes] = jnp.exp(grow) * gate
        if blk == 0:
            end = cum[:, SPAN - 1 : SPAN]
            tail = jnp.transpose(jnp.exp(end - cum) * rate)
            scaled = (expand(tail) * x.astype(F32)).astype(BF)
            bs_ref[...] = dot_tn(scaled, b)
            keep = jnp.transpose(jnp.broadcast_to(jnp.exp(end), (HEADS, SPAN)))
            dec_ref[...] = jnp.transpose(expand(keep))


def mixer_local(x, z, step_t, decay, skip, b, c):
    tok = x.shape[0]
    return pl.pallas_call(
        mixer_local_kernel,
        grid=(REQ,),
        in_specs=[
            pl.BlockSpec((SUF, CH), lambda i: (i, 0)),
            pl.BlockSpec((SUF, CH), lambda i: (i, 0)),
            pl.BlockSpec((HEADS, SUF), lambda i: (0, i)),
            pl.BlockSpec((HEADS, 1), lambda i: (0, 0)),
            pl.BlockSpec((1, CH), lambda i: (0, 0)),
            pl.BlockSpec((SUF, STATE), lambda i: (i, 0)),
            pl.BlockSpec((SUF, STATE), lambda i: (i, 0)),
        ],
        out_specs=[
            pl.BlockSpec((SUF, CH), lambda i: (i, 0)),
            pl.BlockSpec((SUF, CH), lambda i: (i, 0)),
            pl.BlockSpec((None, CH, STATE), lambda i: (i, 0, 0)),
            pl.BlockSpec((None, CH, SPAN), lambda i: (i, 0, 0)),
        ],
        out_shape=[
            jax.ShapeDtypeStruct((tok, CH), F32),
            jax.ShapeDtypeStruct((tok, CH), F32),
            jax.ShapeDtypeStruct((REQ, CH, STATE), F32),
            jax.ShapeDtypeStruct((REQ, CH, SPAN), F32),
        ],
        compiler_params=pltpu.CompilerParams(vmem_limit_bytes=24 << 20),
        cost_estimate=pl.CostEstimate(flops=2_000_000_000, bytes_accessed=11 << 20, transcendentals=2 << 20),
        name="mixer_local",
    )(x, z, step_t, decay, skip, b, c)


def mixer_state_kernel(s_ref, c_ref, p_ref, e_ref, bs_ref, dec_ref, g_ref, sq_ref):
    start = s_ref[...].reshape(CH, STATE)
    dec = dec_ref[...]
    begin = jnp.concatenate([dec, dec], axis=1) * start.astype(F32) + bs_ref[...]
    sums = []
    for blk, state in enumerate((start, begin.astype(BF))):
        rows = pl.ds(blk * SPAN, SPAN)
        carried = dot_nt(c_ref[rows, :], state)
        gated = p_ref[rows, :] + e_ref[rows, :] * carried
        g_ref[rows, :] = gated
        sums.append(jnp.sum(gated * gated, axis=1, keepdims=True))
    sq_ref[...] = jnp.concatenate(sums, axis=0)


def mixer_state(states, c, p, e, bs, dec):
    tok = c.shape[0]
    return pl.pallas_call(
        mixer_state_kernel,
        grid=(REQ,),
        in_specs=[
            pl.BlockSpec((16, None, CH // 16, STATE), lambda i: (0, i, 0, 0)),
            pl.BlockSpec((SUF, STATE), lambda i: (i, 0)),
            pl.BlockSpec((SUF, CH), lambda i: (i, 0)),
            pl.BlockSpec((SUF, CH), lambda i: (i, 0)),
            pl.BlockSpec((None, CH, STATE), lambda i: (i, 0, 0)),
            pl.BlockSpec((None, CH, SPAN), lambda i: (i, 0, 0)),
        ],
        out_specs=[
            pl.BlockSpec((SUF, CH), lambda i: (i, 0)),
            pl.BlockSpec((SUF, 1), lambda i: (i, 0)),
        ],
        out_shape=[
            jax.ShapeDtypeStruct((tok, CH), F32),
            jax.ShapeDtypeStruct((tok, 1), F32),
        ],
        compiler_params=pltpu.CompilerParams(vmem_limit_bytes=24 << 20),
        cost_estimate=pl.CostEstimate(flops=600_000_000, bytes_accessed=11 << 20, transcendentals=0),
        name="mixer_state",
    )(states, c, p, e, bs, dec)


def attend_kernel(pre_ref, suf_ref, base_ref, q_ref, kv_ref, ks_ref, vs_ref, o_ref):
    req = base_ref[0]
    keys = MAXP * PAGE
    q = q_ref[...]
    kv = kv_ref[...].reshape(4 * MAXP, 2 * QUARTER, HD)
    k = kv[:, :QUARTER, :].reshape(keys, HD)
    v = kv[:, QUARTER:, :].reshape(keys, HD)
    scale = 1.0 / math.sqrt(HD)
    s_pre = dot_nt(q, k) * scale
    s_suf = dot_nt(q, ks_ref[...]) * scale
    page = (lax.broadcasted_iota(jnp.int32, (1, keys), 1) // QUARTER) % MAXP
    s_pre = jnp.where(page * PAGE < pre_ref[req], s_pre, NEG)
    row = lax.broadcasted_iota(jnp.int32, (SUF, SUF), 0)
    col = lax.broadcasted_iota(jnp.int32, (SUF, SUF), 1)
    s_suf = jnp.where(row >= col, s_suf, NEG)
    top = jnp.maximum(
        jnp.max(s_pre, axis=1, keepdims=True), jnp.max(s_suf, axis=1, keepdims=True)
    )
    w_pre = jnp.exp(s_pre - top)
    w_suf = jnp.exp(s_suf - top)
    total = jnp.sum(w_pre, axis=1, keepdims=True) + jnp.sum(w_suf, axis=1, keepdims=True)
    mixed = dot_nn(w_pre.astype(BF), v) + dot_nn(w_suf.astype(BF), vs_ref[...])
    out = mixed / total
    live = lax.broadcasted_iota(jnp.int32, (SUF, HD), 0) < suf_ref[req]
    o_ref[...] = jnp.where(live, out, 0.0).astype(BF)


def attend(prefix_len, suffix_len, base, q, kv, ks, vs):
    return pl.pallas_call(
        attend_kernel,
        grid_spec=pltpu.PrefetchScalarGridSpec(
            num_scalar_prefetch=3,
            grid=(8,),
            in_specs=[
                pl.BlockSpec((None, SUF, HD), lambda h, *_: (h // 2, 0, h % 2)),
                pl.BlockSpec((4, MAXP, 2 * QUARTER, HD), lambda h, *_: (0, 0, 0, 0)),
                pl.BlockSpec((SUF, HD), lambda h, *_: (0, 0)),
                pl.BlockSpec((SUF, HD), lambda h, *_: (0, 0)),
            ],
            out_specs=pl.BlockSpec((None, SUF, HD), lambda h, *_: (h // 2, 0, h % 2)),
        ),
        out_shape=jax.ShapeDtypeStruct((4, SUF, 2 * HD), BF),
        compiler_params=pltpu.CompilerParams(vmem_limit_bytes=32 << 20),
        cost_estimate=pl.CostEstimate(flops=2_400_000_000, bytes_accessed=3 << 20, transcendentals=5 << 20),
        name="attend",
    )(prefix_len, suffix_len, base, q, kv, ks, vs)


def gather_kernel(count, base_scale, per, own_ref, slot_ref, base_ref, src_ref, dst_ref, sem):
    first = base_ref[0] * base_scale

    def begin(i, carry):
        e = first + i
        pltpu.make_async_copy(src_ref.at[own_ref[e] * per + slot_ref[e]], dst_ref.at[i], sem).start()
        return carry

    lax.fori_loop(0, count, begin, 0)
    pltpu.make_async_copy(src_ref.at[pl.ds(0, count)], dst_ref, sem).wait()


def gather(owner, slot, base, base_scale, per, table, count, name):
    return pl.pallas_call(
        functools.partial(gather_kernel, count, base_scale, per),
        grid_spec=pltpu.PrefetchScalarGridSpec(
            num_scalar_prefetch=3,
            grid=(1,),
            in_specs=[pl.BlockSpec(memory_space=pl.ANY)],
            out_specs=pl.BlockSpec(memory_space=pl.ANY),
            scratch_shapes=[pltpu.SemaphoreType.DMA(())],
        ),
        out_shape=jax.ShapeDtypeStruct((count,) + table.shape[1:], table.dtype),
        cost_estimate=pl.CostEstimate(flops=0, bytes_accessed=2 << 20, transcendentals=0),
        name=name,
    )(owner, slot, base, table)


def body(
    mixer_input,
    step_raw,
    decay_rate,
    skip_gain,
    state_proj,
    queries,
    suffix_kv,
    state_pool,
    page_pool,
    norm_gain,
    hit_owner,
    hit_slot,
    page_owner,
    page_slot,
    prefix_len,
    suffix_len,
):
    owner_index = lax.axis_index("z") * 2 + lax.axis_index("core")
    x_index = lax.axis_index("x")
    y_index = lax.axis_index("y")
    tok = REQ * SUF

    piece = lax.dynamic_slice(
        page_pool, (0, y_index * QUARTER, 0, x_index, 0), (16, QUARTER, 2, 1, HD)
    ).reshape(16, QUARTER, 2, HD)
    piece = jnp.transpose(piece, (0, 2, 1, 3)).reshape(16, 2 * QUARTER, HD)
    pool = lax.all_gather(piece, OWN, axis=0, tiled=True)

    cut = jnp.transpose(state_pool.reshape(4, 16, CH // 16, STATE), (1, 0, 2, 3))
    hop = lax.all_to_all(cut, OWN, split_axis=0, concat_axis=0, tiled=True)

    query = lax.all_to_all(queries.reshape(REQ, SUF, 2 * HD), "y", split_axis=0, concat_axis=0, tiled=True)

    x = mixer_input[:, 0]
    z = mixer_input[:, 1]
    maps = lax.dynamic_slice(state_proj, (0, 0, x_index, 0), (tok, 2, 1, STATE))
    b = maps[:, 0, 0]
    c = maps[:, 1, 0]
    skip = jnp.repeat(skip_gain, MHDIM)[None]
    p, e, bs, dec = mixer_local(x, z, step_raw.T, decay_rate[:, None], skip, b, c)

    zero = jnp.zeros((1,), jnp.int32)
    wanted = gather(
        hit_owner.reshape(-1), hit_slot, zero, 0, 4, hop.reshape(64, CH // 16, STATE), 64, "pick_states"
    )
    states = lax.all_to_all(wanted.reshape(16, REQ, CH // 16, STATE), OWN, split_axis=0, concat_axis=0, tiled=True)

    base = owner_index.astype(jnp.int32).reshape(1)
    mine = gather(
        page_owner.reshape(-1), page_slot.reshape(-1), base, REQ * MAXP, 16, pool, REQ * MAXP, "pick_pages"
    )
    kv = lax.all_to_all(mine.reshape(REQ, MAXP, 2 * QUARTER, HD), "y", split_axis=0, concat_axis=0, tiled=True)
    own_kv = lax.dynamic_slice(
        suffix_kv, (y_index * SUF, 0, x_index, 0), (SUF, 2, 1, HD)
    )
    request = base * REQ + y_index
    mixed = attend(prefix_len, suffix_len, request, query, kv, own_kv[:, 0, 0], own_kv[:, 1, 0])
    attn_out = lax.all_to_all(mixed, "y", split_axis=0, concat_axis=0, tiled=True).reshape(tok, 2 * HD)

    gated, sums = mixer_state(states, c, p, e, bs, dec)
    square = lax.psum(sums.reshape(8, tok // 8), "y").reshape(tok, 1) / GROUP_CH
    my_suffix = lax.dynamic_slice_in_dim(suffix_len, owner_index * REQ, REQ, 0)
    active = (jnp.arange(SUF)[None, :] < my_suffix[:, None]).reshape(-1)
    normed = gated * lax.rsqrt(square + EPSILON) * norm_gain[None, :]
    mamba_out = jnp.where(active[:, None], normed, 0.0).astype(BF)
    return (mamba_out, attn_out)


def solution(mesh):
    grid = Mesh(mesh.devices.reshape(8, 2, 4, 4), ("z", "core", "x", "y"))
    col = ("x", "y")
    return jax.shard_map(
        body,
        mesh=grid,
        in_specs=(
            P(OWN, None, col),
            P(OWN, col),
            P(col),
            P(col),
            P(OWN, None, None, None),
            P(OWN, col),
            P(OWN, None, None, None),
            P(OWN, col, None, None),
            P(OWN, None, None, None, None),
            P(col),
            P(),
            P(),
            P(),
            P(),
            P(),
            P(),
        ),
        out_specs=(P(OWN, col), P(OWN, col)),
        check_vma=False,
    )
```

time: 450 us -> 211 us (0.47); the launches traced: 443 us -> 211 us
  waiting for transfers between devices: 223 us -> 6.73 us
  Pallas kernels: 0 us -> 89.6 us
  local copies, waits for them, and re-layouts: 82.4 us -> 25.4 us
  other arithmetic: 36.9 us -> 1.6 us
  matrix products: 18.6 us -> 0 us
  between operations: 1.13 us -> 14.3 us
  blocking collectives: 67.3 us -> 54.6 us
  starting transfers between devices: 13.7 us -> 18.4 us
    all_to_all x2 -> x4, waiting for transfers between devices: 223 us -> 6.71 us  [the longest x1 6.7 us: body(): lax.all_to_all(mixed, 'y', split_axis=0, concat_axis=0, tiled=True)]
    pallas_call x0 -> x5, Pallas kernels: none -> 89.6 us  [the longest x2 67.2 us: gather(): pl.pallas_call(functools.partial(gather_kernel, count, base_scale, per),...]
    psum x1, blocking collectives: 67.3 us -> 11 us  [body(): square = lax.psum(sums.reshape(8, tok // 8), 'y').reshape(tok, 1) / GROUP_CH]
    all_to_all x0 -> x1, blocking collectives: none -> 43.6 us  [body(): hop = lax.all_to_all(cut, OWN, split_axis=0, concat_axis=0, tiled=True)]
    gather x5 -> x0, local copies, waits for them, and re-layouts: 23.1 us -> none  [the longest x2 10.6 us: bucket_send(): picked = jnp.take(table, wanted, axis=0, mode='clip')]
    dot_general x8 -> x0, matrix products: 18.6 us -> none  [the longest x1 4.74 us: attend(): jnp.einsum('hqm,md->qhd', weight_pre.astype(jnp.bfloat16), value_pre, pre...]
    select_n x4 -> x0, other arithmetic: 15.3 us -> none  [the longest x2 13.1 us: bucket_send(): jnp.where(filled.reshape((-1,) + (1,) * (picked.ndim - 1)), picked, jnp.z...]
    convert_element_type x2 -> x0, local copies, waits for them, and re-layouts: 12.2 us -> none  [the longest x1 6.15 us: mixer_core(): z_heads.astype(jnp.float32)]
  transfers between devices with their start and end apart: 2 -> 5, of which waited for: 2 -> 1; matrix products, arithmetic and copies ran while one was open for 23% -> 9% of each run, Pallas kernels for 0% -> 37%
where the time goes in v1:
time: 211 us
  Pallas kernels  89.6 us (42%)
  blocking collectives  54.6 us (26%)
  local copies, waits for them, and re-layouts  25.4 us (12%)
  starting transfers between devices  18.4 us (9%)
  between operations  14.3 us (7%)
  waiting for transfers between devices  6.73 us (3%)
    pallas_call x2, Pallas kernels, gather(): pl.pallas_call(functools.partial(gather_kernel, count, base_scale, per),...  67.2 us
    all_to_all x1, blocking collectives, body(): hop = lax.all_to_all(cut, OWN, split_axis=0, concat_axis=0, tiled=True)  43.6 us
    pallas_call x1, Pallas kernels, attend(): pl.pallas_call(attend_kernel, grid_spec=pltpu.PrefetchScalarGridSpec(num_...  11.9 us
    psum x1, blocking collectives, body(): square = lax.psum(sums.reshape(8, tok // 8), 'y').reshape(tok, 1) / GROUP_CH  11 us
    pallas_call x1, Pallas kernels, mixer_local(): pl.pallas_call(mixer_local_kernel, grid=(REQ,), in_specs=[pl.BlockSpec((S...  8.77 us
    slice x1, local copies, waits for them, and re-layouts, body(): z = mixer_input[:, 1]  6.91 us
    all_to_all x1, waiting for transfers between devices, body(): lax.all_to_all(mixed, 'y', split_axis=0, concat_axis=0, tiled=True)  6.7 us
    unnamed x34, local copies, waits for them, and re-layouts  6.3 us
  transfers between devices with their start and end apart: 5, of which 1 were waited for; matrix products, arithmetic and copies ran while one was open for 9% of the time, Pallas kernels for 37%

profile of v1, /device:TPU:6, one launch (start us, length us, event | category | flops | bytes accessed | tf_op | source)
XLA Modules:
  0.0 210.6 jit_solution(9447190024070360543)
XLA Ops:
  7.2 0.0 copy-start.8
  7.2 0.0 all-gather.2.cloned.1.call-start
  7.2 1.9 constant_dynamic-slice_fusion.3
  9.2 0.8 copy.47
  9.9 0.0 all-gather.2.cloned.1.call-update
  9.9 0.0 copy-done.8
  10.0 0.1 copy.58
  10.1 43.6 %all_to_all.25 = bf16[16,4,32,256]{3,2,1,0:T(8,128)(2,1)} all-to-all(bf16[16,4,32,256]{3,2,1,0:T(8,128)(2,1)S(1)} %bitcast.44), channel_id=1, replica_groups=mesh['z'=8,'core'=2,'x'=4,'y'=4] {'z','core'}, dimensions={0} | all-to-all | bytes 2097152 | tf_op jit(solution)/shard_map/all_to_all | solution.py:281
  53.7 4.5 %all-to-all-start.2 = ((bf16[4,256,256]{2,1,0:T(8,128)(2,1)}), bf16[4,256,256]{2,1,0:T(8,128)(2,1)S(1)}, u32[]{:S(2)}, u32[]{:S(2)}) async-start(bf16[4,256,256]{2,1,0:T(8,128)(2,1)} %bitcast.14), calls=%async_computation.2 | async-start | bytes 1048576 | tf_op jit(solution)/shard_map/all_to_all | solution.py:283
  58.2 33.5 %pick_states.1 = bf16[64,32,256]{2,1,0:T(8,128)(2,1)} custom-call(s32[64]{0:T(128)} %bitcast.50, s32[64]{0:T(128)} %slot_ref.1, s32[1]{0:T(128)} %constant.16.clone.1.base_ref, bf16[64,32,256]{2,1,0:T(8,128)(2,1)} %bitcast.43), custom_call_target="tpu_custom_call" | custom-call | bytes 2097152 | tf_op jit(solution)/shard_map/pick_states/pallas_call | solution.py:236
  91.7 0.0 all-to-all-done.2.q_ref
  91.7 0.0 copy-start.2
  91.8 0.8 copy-done.2
  92.5 5.5 %all-to-all-start.1 = ((bf16[16,4,32,256]{3,2,1,0:T(8,128)(2,1)}), bf16[16,4,32,256]{3,2,1,0:T(8,128)(2,1)S(1)}, u32[]{:S(2)}, u32[]{:S(2)}) async-start(bf16[16,4,32,256]{3,2,1,0:T(8,128)(2,1)} %bitcast.42), calls=%async_computation.1 | async-start | bytes 2097152 | tf_op jit(solution)/shard_map/all_to_all | solution.py:297
  98.1 4.4 %constant_dynamic-slice_fusion.4 = (bf16[1024,1,1,256]{3,2,1,0:T(2,128)(2,1)S(1)}, bf16[1024,1,1,256]{3,2,1,0:T(2,128)(2,1)S(1)}) fusion(bf16[1024,2,4,256]{3,2,1,0:T(4,128)(2,1)} %param.20, s32[]{:T(128)S(6)} %select_n.19, s32[]{:T(128)S(6)} %add.47), kind=kLoop, calls=%fused_computation.14 | loop fusion | bytes 2097160 | tf_op jit(solution)/shard_map/slice | solution.py:288
  102.5 0.0 copy-start.12
  102.5 0.0 copy-start.13
  102.5 0.0 copy-start.6
  102.5 0.0 copy-start.9
  102.5 0.0 copy-start.10
  102.5 0.1 copy.60
  102.6 0.1 copy.59
  102.7 0.4 copy-done.12
  103.1 0.1 broadcast_in_dim.23
  103.2 0.1 broadcast_in_dim_reshape.4.skip_ref
  103.3 0.0 copy-done.13
  103.3 0.1 copy.37.decay_ref
  103.4 0.0 copy-done.6
  103.4 0.1 dynamic_slice.12
  103.4 0.1 iota_compare_fusion
  103.5 0.0 copy-done.9
  103.5 0.1 copy.38
  103.6 0.7 reshape.83.own_ref
  104.3 0.0 copy-done.10
  104.3 0.1 copy.39
  104.4 0.7 reshape.84.slot_ref
  105.0 1.3 constant_dynamic-slice_fusion.2
  106.3 6.9 %fusion = (bf16[1024,1,512]{2,1,0:T(2,128)(2,1)}, bf16[1024,1,512]{2,1,0:T(2,128)(2,1)}) fusion(bf16[1024,2,512]{2,1,0:T(2,128)(2,1)} %param.16), kind=kLoop, calls=%fused_computation.15 | loop fusion | bytes 4194304 | tf_op jit(solution)/shard_map/slice | solution.py:286
  113.3 0.0 all-gather.2.cloned.1.call-done.src_ref
  113.3 33.7 %pick_pages.1 = bf16[64,64,128]{2,1,0:T(8,128)(2,1)} custom-call(s32[1024]{0:T(1024)} %reshape.83.own_ref, s32[1024]{0:T(1024)} %reshape.84.slot_ref, s32[1]{0:T(128)} %bitcast.12.base_ref, bf16[256,64,128]{2,1,0:T(8,128)(2,1)} %all-gather.2.cloned.1.call-done.src_ref), custom_call_target="tpu_custom_call" | custom-call | bytes 2097152 | tf_op jit(solution)/shard_map/pick_pages/pallas_call | solution.py:236
  146.9 0.0 all-to-all-done.1.s_ref
  146.9 4.8 %all-to-all-start.3 = ((bf16[4,16,64,128]{3,2,1,0:T(8,128)(2,1)}), bf16[4,16,64,128]{3,2,1,0:T(8,128)(2,1)S(1)}, u32[]{:S(2)}, u32[]{:S(2)}) async-start(bf16[4,16,64,128]{3,2,1,0:T(8,128)(2,1)} %bitcast.45), calls=%async_computation.3 | async-start | bytes 2097152 | tf_op jit(solution)/shard_map/all_to_all | solution.py:303
  151.8 2.8 %copy_bitcast_fusion = (bf16[1024,512]{1,0:T(8,128)(2,1)S(1)}, bf16[1024,512]{1,0:T(8,128)(2,1)S(1)}) fusion(bf16[1024,1,512]{2,1,0:T(2,128)(2,1)} %get-tuple-element.18, bf16[1024,1,512]{2,1,0:T(2,128)(2,1)} %get-tuple-element.19), kind=kLoop, calls=%fused_computation.1 | loop fusion | bytes 4194304 | tf_op jit(solution)/shard_map/squeeze | solution.py:286
  154.6 0.0 copy-done.5
  154.6 8.8 %mixer_local.1 = (f32[1024,512]{1,0:T(8,128)S(1)}, f32[1024,512]{1,0:T(8,128)S(1)}, f32[4,512,256]{2,1,0:T(8,128)S(1)}, f32[4,512,128]{2,1,0:T(8,128)S(1)}) custom-call(bf16[1024,512]{1,0:T(8,128)(2,1)S(1)} %get-tuple-element.21.x_ref, bf16[1024,512]{1,0:T(8,128)(2,1)S(1)} %get-tuple-element.20.z_ref, f32[8,1024]{1,0:T(8,128)S(1)} %bitcast.41, ...), custom_call_target="tpu_custom_call" | custom-call | flops 2000000000 | bytes 11534336 | tf_op jit(solution)/shard_map/mixer_local/pallas_call | solution.py:104
  163.4 0.0 copy-start.7
  163.4 1.7 mixer_state.1
  165.1 0.0 copy-start
  165.1 1.3 copy-done
  166.4 0.2 reduce
  166.6 11.0 %psum.7 = f32[8,128]{1,0:T(8,128)S(1)} all-reduce(f32[8,128]{1,0:T(8,128)S(1)} %bitcast.49), channel_id=1, replica_groups=mesh['z'=8,'core'=2,'x'=4,'y'=4] {'y'}, use_global_device_ids=true, to_apply=%region_0.0 | all-reduce | flops 1024 | bytes 8192 | tf_op jit(solution)/shard_map/psum | solution.py:312
  177.6 0.0 all-to-all-done.3.kv_ref
  177.6 0.0 copy-done.7
  177.6 0.0 copy-start.3
  177.6 1.0 copy-done.3
  178.7 11.9 %attend.1 = bf16[4,256,256]{2,1,0:T(8,128)(2,1)S(1)} custom-call(s32[64]{0:T(128)S(1)} %copy-done.7, s32[64]{0:T(128)S(1)} %copy-done.6, s32[1]{0:T(128)S(6)} %add.43.base_ref, bf16[4,256,256]{2,1,0:T(8,128)(2,1)S(1)} %copy-done.3, bf16[4,16,64,128]{3,2,1,0:T(8,128)(2,1)S(1)} %all-to-all-done.3.kv_ref, bf16[256,128]{1,0:T(8,128)(2,1)S(1)} %get-tuple-element.23.ks_ref, ...), custom_call_target="tpu_custom_call" | custom-call | flops 2400000000 | bytes 3145728 | tf_op jit(solution)/shard_map/attend/pallas_call | solution.py:203
  190.6 0.0 copy-start.4
  190.6 0.8 copy-done.4
  191.4 3.5 %all-to-all-start.4 = ((bf16[4,256,256]{2,1,0:T(8,128)(2,1)}), bf16[4,256,256]{2,1,0:T(8,128)(2,1)S(1)}, u32[]{:S(2)}, u32[]{:S(2)}) async-start(bf16[4,256,256]{2,1,0:T(8,128)(2,1)} %copy-done.4), calls=%async_computation.4 | async-start | bytes 1048576 | tf_op jit(solution)/shard_map/all_to_all | solution.py:309
  194.9 0.0 copy-done.1
  194.9 0.0 copy-done.11
  194.9 1.3 select_convert_fusion
  196.2 6.7 %all-to-all-done.4 = bf16[4,256,256]{2,1,0:T(8,128)(2,1)S(1)} async-done(((bf16[4,256,256]{2,1,0:T(8,128)(2,1)}), bf16[4,256,256]{2,1,0:T(8,128)(2,1)S(1)}, u32[]{:S(2)}, u32[]{:S(2)}) %all-to-all-start.4) | async-done | bytes 524320 | tf_op jit(solution)/shard_map/all_to_all | solution.py:309
  202.9 0.8 copy.62
  (6 shorter events, 0.0 us)
Async XLA Ops:
  7.2 2.8 %copy-start.8 = (bf16[4,8,64,256]{3,2,1,0:T(8,128)(2,1)S(1)}, bf16[4,8,64,256]{3,2,1,0:T(8,128)(2,1)}, u32[]{:S(2)}) copy-start(bf16[4,8,64,256]{3,2,1,0:T(8,128)(2,1)} %param.23) | copy-start | bytes 3145732
  7.2 106.1 %all-gather.2.cloned.1.call-start = ((), (), s32[]{:S(2)}) async-start(), calls=%async_computation.5 | async-start | bytes 4456448 | tf_op jit(solution)/shard_map/all_gather | solution.py:278
  53.7 38.1 %all-to-all-start.2 = ((bf16[4,256,256]{2,1,0:T(8,128)(2,1)}), bf16[4,256,256]{2,1,0:T(8,128)(2,1)S(1)}, u32[]{:S(2)}, u32[]{:S(2)}) async-start(bf16[4,256,256]{2,1,0:T(8,128)(2,1)} %bitcast.14), calls=%async_computation.2 | async-start | bytes 1048576 | tf_op jit(solution)/shard_map/all_to_all | solution.py:283
  91.7 0.8 copy-start.2
  92.5 54.4 %all-to-all-start.1 = ((bf16[16,4,32,256]{3,2,1,0:T(8,128)(2,1)}), bf16[16,4,32,256]{3,2,1,0:T(8,128)(2,1)S(1)}, u32[]{:S(2)}, u32[]{:S(2)}) async-start(bf16[16,4,32,256]{3,2,1,0:T(8,128)(2,1)} %bitcast.42), calls=%async_computation.1 | async-start | bytes 2097152 | tf_op jit(solution)/shard_map/all_to_all | solution.py:297
  102.5 0.7 copy-start.12
  102.5 0.8 copy-start.13
  102.5 0.9 copy-start.6
  102.5 1.0 copy-start.9
  102.5 1.8 copy-start.10
  146.9 30.7 %all-to-all-start.3 = ((bf16[4,16,64,128]{3,2,1,0:T(8,128)(2,1)}), bf16[4,16,64,128]{3,2,1,0:T(8,128)(2,1)S(1)}, u32[]{:S(2)}, u32[]{:S(2)}) async-start(bf16[4,16,64,128]{3,2,1,0:T(8,128)(2,1)} %bitcast.45), calls=%async_computation.3 | async-start | bytes 2097152 | tf_op jit(solution)/shard_map/all_to_all | solution.py:303
  151.8 2.8 %copy-start.5 = (f32[1024,8]{0,1:T(8,128)S(1)}, f32[1024,8]{0,1:T(8,128)}, u32[]{:S(2)}) copy-start(f32[1024,8]{0,1:T(8,128)} %param.17) | copy-start | bytes 98308
  163.4 14.2 %copy-start.7 = (s32[64]{0:T(128)S(1)}, s32[64]{0:T(128)}, u32[]{:S(2)}) copy-start(s32[64]{0:T(128)} %pre_ref.1) | copy-start | bytes 772
  165.1 1.3 copy-start
  177.6 1.0 copy-start.3
  178.7 16.2 %copy-start.1 = (f32[1024,512]{1,0:T(8,128)S(1)}, f32[1024,512]{1,0:T(8,128)}, u32[]{:S(2)}) copy-start(f32[1024,512]{1,0:T(8,128)} %copy-done) | copy-start | bytes 6291460
  178.7 16.2 %copy-start.11 = (f32[512]{0:T(512)S(1)}, f32[512]{0:T(512)}, u32[]{:S(2)}) copy-start(f32[512]{0:T(512)} %param.25) | copy-start | bytes 6148
  190.6 0.8 copy-start.4
  191.4 11.5 %all-to-all-start.4 = ((bf16[4,256,256]{2,1,0:T(8,128)(2,1)}), bf16[4,256,256]{2,1,0:T(8,128)(2,1)S(1)}, u32[]{:S(2)}, u32[]{:S(2)}) async-start(bf16[4,256,256]{2,1,0:T(8,128)(2,1)} %copy-done.4), calls=%async_computation.4 | async-start | bytes 1048576 | tf_op jit(solution)/shard_map/all_to_all | solution.py:309
Sparse Core Ops, SparseCore 0:
  10.1 60.0 all-gather.1

commit v2 on v1

v2 whole, which is shorter than its diff:
```python
import functools
import math

import jax
import jax.numpy as jnp
from jax import lax
from jax.experimental import pallas as pl
from jax.experimental.pallas import tpu as pltpu
from jax.sharding import Mesh
from jax.sharding import PartitionSpec as P

HEADS = 8
MHDIM = 64
CH = HEADS * MHDIM
STATE = 256
GROUP_CH = 2048
HD = 128
PAGE = 128
SPAN = 128
SUF = 256
MAXP = 16
REQ = 4
QUARTER = PAGE // 4
EPSILON = 1e-05
NEG = -1e30
OWN = ("z", "core")
BF = jnp.bfloat16
F32 = jnp.float32
HI = lax.Precision.HIGHEST


def dot_nt(a, b):
    return lax.dot_general(a, b, (((1,), (1,)), ((), ())), preferred_element_type=F32)


def dot_nn(a, b):
    return lax.dot_general(a, b, (((1,), (0,)), ((), ())), preferred_element_type=F32)


def dot_tn(a, b):
    return lax.dot_general(a, b, (((0,), (0,)), ((), ())), preferred_element_type=F32)


def expand(cols):
    head = lax.broadcasted_iota(jnp.int32, (HEADS, CH), 0)
    chan = lax.broadcasted_iota(jnp.int32, (HEADS, CH), 1)
    pick = (chan // MHDIM == head).astype(F32)
    return lax.dot_general(
        cols, pick, (((1,), (0,)), ((), ())), preferred_element_type=F32, precision=HI
    )


def mixer_local_kernel(x_ref, z_ref, step_ref, decay_ref, skip_ref, b_ref, c_ref, p_ref, e_ref, bs_ref, dec_ref):
    lane = lax.broadcasted_iota(jnp.int32, (HEADS, SPAN), 1)
    row = lax.broadcasted_iota(jnp.int32, (SPAN, SPAN), 0)
    col = lax.broadcasted_iota(jnp.int32, (SPAN, SPAN), 1)
    lower = row >= col
    low_half = lax.broadcasted_iota(jnp.int32, (SPAN, 2 * MHDIM), 1) < MHDIM
    for blk in range(SUF // SPAN):
        rows = pl.ds(blk * SPAN, SPAN)
        raw = step_ref[:, rows]
        rate = jnp.maximum(raw, 0.0) + jnp.log(1.0 + jnp.exp(-jnp.abs(raw)))
        cum = -rate * decay_ref[...]
        shift = 1
        while shift < SPAN:
            cum = cum + jnp.where(lane >= shift, pltpu.roll(cum, shift, 1), 0.0)
            shift *= 2
        cum_col = jnp.transpose(cum)
        x = x_ref[rows, :]
        b = b_ref[rows, :]
        c = c_ref[rows, :]
        inter = dot_nt(c, b)
        for pair in range(HEADS // 2):
            parts = []
            for h in (2 * pair, 2 * pair + 1):
                gap = cum_col[:, h : h + 1] - cum[h : h + 1, :]
                fade = jnp.exp(jnp.where(lower, gap, NEG))
                parts.append((inter * fade * rate[h : h + 1, :]).astype(BF))
            lanes = pl.ds(pair * 2 * MHDIM, 2 * MHDIM)
            xp = x_ref[rows, lanes]
            first = dot_nn(parts[0], xp)
            second = dot_nn(parts[1], xp)
            inner = jnp.where(low_half, first, second)
            z = z_ref[rows, lanes].astype(F32)
            gate = z / (1.0 + jnp.exp(-z))
            p_ref[rows, lanes] = (inner + skip_ref[:, lanes] * xp.astype(F32)) * gate
            grow = jnp.where(
                low_half,
                jnp.broadcast_to(cum_col[:, 2 * pair : 2 * pair + 1], (SPAN, 2 * MHDIM)),
                jnp.broadcast_to(cum_col[:, 2 * pair + 1 : 2 * pair + 2], (SPAN, 2 * MHDIM)),
            )
            e_ref[rows, lanes] = jnp.exp(grow) * gate
        if blk == 0:
            end = cum[:, SPAN - 1 : SPAN]
            tail = jnp.transpose(jnp.exp(end - cum) * rate)
            scaled = (expand(tail) * x.astype(F32)).astype(BF)
            bs_ref[...] = dot_tn(scaled, b)
            keep = jnp.transpose(jnp.broadcast_to(jnp.exp(end), (HEADS, SPAN)))
            dec_ref[...] = jnp.transpose(expand(keep))


def mixer_local(x, z, step_t, decay, skip, b, c):
    tok = x.shape[0]
    return pl.pallas_call(
        mixer_local_kernel,
        grid=(REQ,),
        in_specs=[
            pl.BlockSpec((SUF, CH), lambda i: (i, 0)),
            pl.BlockSpec((SUF, CH), lambda i: (i, 0)),
            pl.BlockSpec((HEADS, SUF), lambda i: (0, i)),
            pl.BlockSpec((HEADS, 1), lambda i: (0, 0)),
            pl.BlockSpec((1, CH), lambda i: (0, 0)),
            pl.BlockSpec((SUF, STATE), lambda i: (i, 0)),
            pl.BlockSpec((SUF, STATE), lambda i: (i, 0)),
        ],
        out_specs=[
            pl.BlockSpec((SUF, CH), lambda i: (i, 0)),
            pl.BlockSpec((SUF, CH), lambda i: (i, 0)),
            pl.BlockSpec((None, CH, STATE), lambda i: (i, 0, 0)),
            pl.BlockSpec((None, CH, SPAN), lambda i: (i, 0, 0)),
        ],
        out_shape=[
            jax.ShapeDtypeStruct((tok, CH), F32),
            jax.ShapeDtypeStruct((tok, CH), F32),
            jax.ShapeDtypeStruct((REQ, CH, STATE), F32),
            jax.ShapeDtypeStruct((REQ, CH, SPAN), F32),
        ],
        compiler_params=pltpu.CompilerParams(vmem_limit_bytes=24 << 20),
        cost_estimate=pl.CostEstimate(flops=2_000_000_000, bytes_accessed=11 << 20, transcendentals=2 << 20),
        name="mixer_local",
    )(x, z, step_t, decay, skip, b, c)


MESH = pl.DeviceIdType.MESH


def attend_pair(q_ref, k, v, ks, vs, bias, causal, live, o_ref, slot):
    scale = 1.0 / math.sqrt(HD)
    for half in range(2):
        lanes = pl.ds(half * HD, HD)
        q = q_ref[slot, :, lanes]
        s_pre = dot_nt(q, k) * scale + bias
        s_suf = jnp.where(causal, dot_nt(q, ks) * scale, NEG)
        top = jnp.maximum(
            jnp.max(s_pre, axis=1, keepdims=True), jnp.max(s_suf, axis=1, keepdims=True)
        )
        w_pre = jnp.exp(s_pre - top)
        w_suf = jnp.exp(s_suf - top)
        total = jnp.sum(w_pre, axis=1, keepdims=True) + jnp.sum(w_suf, axis=1, keepdims=True)
        mixed = dot_nn(w_pre.astype(BF), v) + dot_nn(w_suf.astype(BF), vs)
        o_ref[slot, :, lanes] = jnp.where(live, mixed / total, 0.0).astype(BF)


def finish_kernel(
    pre_ref,
    suf_ref,
    want_ref,
    page_ref,
    q_ref,
    ks_ref,
    vs_ref,
    c_ref,
    p_ref,
    e_ref,
    bs_ref,
    dec_ref,
    gain_ref,
    mamba_ref,
    attn_ref,
    st_buf,
    kv_buf,
    o_buf,
    gated_buf,
    sum_buf,
    st_send,
    st_recv,
    kv_send,
    kv_recv,
    o_send,
    o_recv,
    sum_send,
    sum_recv,
):
    y = lax.axis_index("y")
    me = lax.axis_index("z") * 2 + lax.axis_index("core")

    barrier = pltpu.get_barrier_semaphore()

    def owner_id(k):
        other = lax.rem(me + k, 16)
        return other, {"z": other // 2, "core": lax.rem(other, 2)}

    def y_id(k):
        other = lax.rem(y + k, 4)
        return other, {"y": other}

    def greet(k, carry):
        pl.semaphore_signal(barrier, inc=1, device_id=owner_id(k)[1], device_id_type=MESH)
        return carry

    lax.fori_loop(1, 16, greet, 0)
    for k in range(1, 4):
        pl.semaphore_signal(barrier, inc=1, device_id=y_id(k)[1], device_id_type=MESH)
    pl.semaphore_wait(barrier, 18)

    def state_copy(k):
        other, device = owner_id(k)
        return pltpu.make_async_remote_copy(
            want_ref.at[other], st_buf.at[me], st_send.at[k], st_recv.at[k], device_id=device, device_id_type=MESH
        )

    def page_copy(k):
        other, device = y_id(k)
        return pltpu.make_async_remote_copy(
            page_ref.at[other], kv_buf.at[y], kv_send.at[k], kv_recv.at[k], device_id=device, device_id_type=MESH
        )

    def out_copy(k):
        other, device = y_id(k)
        return pltpu.make_async_remote_copy(
            o_buf.at[other], attn_ref.at[y], o_send.at[k], o_recv.at[k], device_id=device, device_id_type=MESH
        )

    def sum_copy(k):
        device = y_id(k)[1]
        return pltpu.make_async_remote_copy(
            sum_buf.at[y], sum_buf.at[y], sum_send.at[k], sum_recv.at[k], device_id=device, device_id_type=MESH
        )

    for k in (2, 1, 3):
        page_copy(k).start()

    def send_state(k, carry):
        state_copy(k).start()
        return carry

    lax.fori_loop(1, 16, send_state, 0)
    kv_buf[y] = page_ref[y]
    st_buf[me] = want_ref[me]
    for k in (1, 2, 3):
        page_copy(k).wait()

    request = me * REQ + y
    keys = MAXP * PAGE
    page = (lax.broadcasted_iota(jnp.int32, (1, keys), 1) // QUARTER) % MAXP
    bias = jnp.where(page * PAGE < pre_ref[request], 0.0, NEG)
    causal = lax.broadcasted_iota(jnp.int32, (SUF, SUF), 0) >= lax.broadcasted_iota(jnp.int32, (SUF, SUF), 1)
    live = lax.broadcasted_iota(jnp.int32, (SUF, HD), 0) < suf_ref[request]

    def attend_step(t, carry):
        kv = kv_buf[...].reshape(4 * MAXP, 2 * QUARTER, HD)
        k = kv[:, :QUARTER, :].reshape(keys, HD)
        v = kv[:, QUARTER:, :].reshape(keys, HD)
        slot = lax.rem(y + t, 4)
        attend_pair(q_ref, k, v, ks_ref[...], vs_ref[...], bias, causal, live, o_buf, slot)
        return carry

    lax.fori_loop(1, 5, attend_step, 0)
    for k in (1, 2, 3):
        out_copy(k).start()
    attn_ref[y] = o_buf[y]

    def wait_state(k, carry):
        state_copy(k).wait()
        return carry

    lax.fori_loop(1, 16, wait_state, 0)

    def mixer_step(j, carry):
        start = st_buf[:, j].reshape(CH, STATE)
        dec = dec_ref[j]
        begin = jnp.concatenate([dec, dec], axis=1) * start.astype(F32) + bs_ref[j]
        for blk, state in enumerate((start, begin.astype(BF))):
            rows = pl.ds(pl.multiple_of(j * SUF + blk * SPAN, SPAN), SPAN)
            carried = dot_nt(c_ref[rows, :], state)
            gated = p_ref[rows, :] + e_ref[rows, :] * carried
            gated_buf[rows, :] = gated
            total = jnp.sum(gated * gated, axis=1, keepdims=True)
            sum_buf[y, pl.ds(2 * j + blk, 1), :] = jnp.transpose(jnp.broadcast_to(total, (SPAN, SPAN)))[0:1, :]
        return carry

    lax.fori_loop(0, REQ, mixer_step, 0)
    for k in (2, 1, 3):
        sum_copy(k).start()
    for k in (1, 2, 3):
        sum_copy(k).wait()

    def norm_step(i, carry):
        rows = pl.ds(pl.multiple_of(i * SPAN, SPAN), SPAN)
        square = jnp.sum(sum_buf[:, pl.ds(i, 1), :], axis=0) / GROUP_CH
        factor = jnp.transpose(jnp.broadcast_to(lax.rsqrt(square + EPSILON), (SPAN, SPAN)))
        token = lax.broadcasted_iota(jnp.int32, (SPAN, SPAN), 0) + lax.rem(i, 2) * SPAN
        alive = token < suf_ref[me * REQ + i // 2]
        for part in range(CH // SPAN):
            lanes = pl.ds(part * SPAN, SPAN)
            value = gated_buf[rows, lanes] * factor * gain_ref[:, lanes]
            mamba_ref[rows, lanes] = jnp.where(alive, value, 0.0).astype(BF)
        return carry

    lax.fori_loop(0, 8, norm_step, 0)
    for k in (1, 2, 3):
        out_copy(k).wait()


def finish(prefix_len, suffix_len, wanted, mine, q, ks, vs, c, p, e, bs, dec, gain):
    vmem = pl.BlockSpec(memory_space=pltpu.VMEM)
    smem = pl.BlockSpec(memory_space=pltpu.SMEM)
    dma = pltpu.SemaphoreType.DMA
    return pl.pallas_call(
        finish_kernel,
        in_specs=[smem, smem] + [vmem] * 11,
        out_specs=[vmem, vmem],
        out_shape=[
            jax.ShapeDtypeStruct((REQ * SUF, CH), BF),
            jax.ShapeDtypeStruct((4, SUF, 2 * HD), BF),
        ],
        scratch_shapes=[
            pltpu.VMEM((16, REQ, CH // 16, STATE), BF),
            pltpu.VMEM((4, MAXP, 2 * QUARTER, HD), BF),
            pltpu.VMEM((4, SUF, 2 * HD), BF),
            pltpu.VMEM((REQ * SUF, CH), F32),
            pltpu.VMEM((4, 8, SPAN), F32),
            dma((16,)),
            dma((16,)),
            dma((4,)),
            dma((4,)),
            dma((4,)),
            dma((4,)),
            dma((4,)),
            dma((4,)),
        ],
        compiler_params=pltpu.CompilerParams(
            collective_id=0, has_side_effects=True, vmem_limit_bytes=40 << 20
        ),
        cost_estimate=pl.CostEstimate(flops=3_000_000_000, bytes_accessed=16 << 20, transcendentals=5 << 20),
        name="finish",
    )(prefix_len, suffix_len, wanted, mine, q, ks, vs, c, p, e, bs, dec, gain)


def cut_kernel(src_ref, dst_ref, sem):
    for k in range(16):
        pltpu.make_async_copy(src_ref.at[:, k], dst_ref.at[k], sem.at[k]).start()
    for k in range(16):
        pltpu.make_async_copy(src_ref.at[:, k], dst_ref.at[k], sem.at[k]).wait()


def cut_states(states):
    return pl.pallas_call(
        cut_kernel,
        in_specs=[pl.BlockSpec(memory_space=pltpu.VMEM)],
        out_specs=pl.BlockSpec(memory_space=pltpu.HBM),
        out_shape=jax.ShapeDtypeStruct((16, 4, CH // 16, STATE), BF),
        scratch_shapes=[pltpu.SemaphoreType.DMA((16,))],
        cost_estimate=pl.CostEstimate(flops=0, bytes_accessed=2 << 20, transcendentals=0),
        name="cut_states",
    )(states)


def pick_kernel(ho_ref, hs_ref, po_ref, ps_ref, base_ref, hop_ref, pool_ref, want_ref, mine_ref, sem):
    first = base_ref[0] * REQ * MAXP

    def begin(i, carry):
        pltpu.make_async_copy(hop_ref.at[ho_ref[i] * 4 + hs_ref[i]], want_ref.at[i], sem.at[0]).start()
        e = first + i
        pltpu.make_async_copy(pool_ref.at[po_ref[e] * 16 + ps_ref[e]], mine_ref.at[i], sem.at[1]).start()
        return carry

    lax.fori_loop(0, 64, begin, 0)
    pltpu.make_async_copy(hop_ref.at[pl.ds(0, 64)], want_ref, sem.at[0]).wait()
    pltpu.make_async_copy(pool_ref.at[pl.ds(0, 64)], mine_ref, sem.at[1]).wait()


def pick(hit_owner, hit_slot, page_owner, page_slot, base, hop, pool):
    smem = pl.BlockSpec(memory_space=pltpu.SMEM)
    hbm = pl.BlockSpec(memory_space=pltpu.HBM)
    vmem = pl.BlockSpec(memory_space=pltpu.VMEM)
    return pl.pallas_call(
        pick_kernel,
        in_specs=[smem] * 5 + [hbm, hbm],
        out_specs=[vmem, vmem],
        out_shape=[
            jax.ShapeDtypeStruct((64,) + hop.shape[1:], BF),
            jax.ShapeDtypeStruct((64,) + pool.shape[1:], BF),
        ],
        scratch_shapes=[pltpu.SemaphoreType.DMA((2,))],
        cost_estimate=pl.CostEstimate(flops=0, bytes_accessed=4 << 20, transcendentals=0),
        name="pick",
    )(hit_owner, hit_slot, page_owner, page_slot, base, hop, pool)


def body(
    mixer_input,
    step_raw,
    decay_rate,
    skip_gain,
    state_proj,
    queries,
    suffix_kv,
    state_pool,
    page_pool,
    norm_gain,
    hit_owner,
    hit_slot,
    page_owner,
    page_slot,
    prefix_len,
    suffix_len,
):
    owner_index = lax.axis_index("z") * 2 + lax.axis_index("core")
    x_index = lax.axis_index("x")
    y_index = lax.axis_index("y")
    tok = REQ * SUF

    piece = lax.dynamic_slice(
        page_pool, (0, y_index * QUARTER, 0, x_index, 0), (16, QUARTER, 2, 1, HD)
    ).reshape(16, QUARTER, 2, HD)
    piece = jnp.transpose(piece, (0, 2, 1, 3)).reshape(16, 2 * QUARTER, HD)
    pool = lax.all_gather(piece, OWN, axis=0, tiled=True)

    cut = cut_states(state_pool.reshape(4, 16, CH // 16, STATE))
    hop = lax.all_to_all(cut, OWN, split_axis=0, concat_axis=0, tiled=True)

    query = lax.all_to_all(queries.reshape(REQ, SUF, 2 * HD), "y", split_axis=0, concat_axis=0, tiled=True)

    x = mixer_input[:, 0]
    z = mixer_input[:, 1]
    maps = lax.dynamic_slice(state_proj, (0, 0, x_index, 0), (tok, 2, 1, STATE))
    b = maps[:, 0, 0]
    c = maps[:, 1, 0]
    skip = jnp.repeat(skip_gain, MHDIM)[None]
    p, e, bs, dec = mixer_local(x, z, step_raw.T, decay_rate[:, None], skip, b, c)

    own_kv = lax.dynamic_slice(suffix_kv, (y_index * SUF, 0, x_index, 0), (SUF, 2, 1, HD))

    wanted, mine = pick(
        hit_owner.reshape(-1),
        hit_slot,
        page_owner.reshape(-1),
        page_slot.reshape(-1),
        owner_index.astype(jnp.int32).reshape(1),
        hop.reshape(64, CH // 16, STATE),
        pool,
    )
    mamba_out, attn = finish(
        prefix_len,
        suffix_len,
        wanted.reshape(16, REQ, CH // 16, STATE),
        mine.reshape(REQ, MAXP, 2 * QUARTER, HD),
        query,
        own_kv[:, 0, 0],
        own_kv[:, 1, 0],
        c,
        p,
        e,
        bs,
        dec,
        norm_gain[None],
    )
    return (mamba_out, attn.reshape(tok, 2 * HD))


def solution(mesh):
    grid = Mesh(mesh.devices.reshape(8, 2, 4, 4), ("z", "core", "x", "y"))
    col = ("x", "y")
    return jax.shard_map(
        body,
        mesh=grid,
        in_specs=(
            P(OWN, None, col),
            P(OWN, col),
            P(col),
            P(col),
            P(OWN, None, None, None),
            P(OWN, col),
            P(OWN, None, None, None),
            P(OWN, col, None, None),
            P(OWN, None, None, None, None),
            P(col),
            P(),
            P(),
            P(),
            P(),
            P(),
            P(),
        ),
        out_specs=(P(OWN, col), P(OWN, col)),
        check_vma=False,
    )
```

time: 211 us -> 135 us (0.64)
  blocking collectives: 54.6 us -> 0 us
  Pallas kernels: 89.6 us -> 54.7 us
  waiting for transfers between devices: 6.73 us -> 23.6 us
  starting transfers between devices: 18.4 us -> 13.2 us
  local copies, waits for them, and re-layouts: 25.4 us -> 28.2 us
    all_to_all x1 -> x0, blocking collectives: 43.6 us -> none  [body(): hop = lax.all_to_all(cut, OWN, split_axis=0, concat_axis=0, tiled=True)]
    pallas_call x4 -> x3, Pallas kernels: 80.8 us -> 45.8 us  [the longest x1 39.6 us: finish(): pl.pallas_call(finish_kernel, in_specs=[smem, smem] + [vmem] * 11, out_sp...]
    all_to_all x3 -> x1, waiting for transfers between devices: 6.7 us -> 23.6 us  [body(): hop = lax.all_to_all(cut, OWN, split_axis=0, concat_axis=0, tiled=True)]
    psum x1 -> x0, blocking collectives: 11 us -> none  [body(): square = lax.psum(sums.reshape(8, tok // 8), 'y').reshape(tok, 1) / GROUP_CH]
    unnamed x34 -> x45, local copies, waits for them, and re-layouts: 6.3 us -> 15.4 us
    all_to_all x3 -> x1, starting transfers between devices: 13.8 us -> 8.63 us  [body(): hop = lax.all_to_all(cut, OWN, split_axis=0, concat_axis=0, tiled=True)]
    slice x1, local copies, waits for them, and re-layouts: 6.91 us -> 2.95 us  [body(): z = mixer_input[:, 1]]
    squeeze x1, local copies, waits for them, and re-layouts: 2.83 us -> 0.6 us  [body(): z = mixer_input[:, 1]]
  transfers between devices with their start and end apart: 5 -> 3, of which waited for: 1 -> 1; matrix products, arithmetic and copies ran while one was open for 9% -> 8% of each run, Pallas kernels for 37% -> 11%
where the time goes in v2:
time: 135 us; the launch traced here: 134 us
  Pallas kernels  54.7 us (41%)
  local copies, waits for them, and re-layouts  28.2 us (21%)
  waiting for transfers between devices  23.6 us (17%)
  between operations  14.3 us (11%)
  starting transfers between devices  13.2 us (10%)
    pallas_call x1, Pallas kernels, finish(): pl.pallas_call(finish_kernel, in_specs=[smem, smem] + [vmem] * 11, out_sp...  39.6 us
    all_to_all x1, waiting for transfers between devices, body(): hop = lax.all_to_all(cut, OWN, split_axis=0, concat_axis=0, tiled=True)  23.6 us
    unnamed x45, local copies, waits for them, and re-layouts  15.4 us
    pallas_call x1, Pallas kernels, mixer_local(): pl.pallas_call(mixer_local_kernel, grid=(REQ,), in_specs=[pl.BlockSpec((S...  8.81 us
    all_to_all x1, starting transfers between devices, body(): hop = lax.all_to_all(cut, OWN, split_axis=0, concat_axis=0, tiled=True)  8.63 us
    all_to_all x1, starting transfers between devices, body(): lax.all_to_all(queries.reshape(REQ, SUF, 2 * HD), 'y', split_axis=0, conc...  4.51 us
    slice x1, local copies, waits for them, and re-layouts, body(): b = maps[:, 0, 0]  4.42 us
    pallas_call x1, Pallas kernels, pick(): pl.pallas_call(pick_kernel, in_specs=[smem] * 5 + [hbm, hbm], out_specs=[...  3.88 us
  transfers between devices with their start and end apart: 3, of which 1 were waited for; matrix products, arithmetic and copies ran while one was open for 8% of the time, Pallas kernels for 11%

profile of v2, /device:TPU:6, one launch (start us, length us, event | category | flops | bytes accessed | tf_op | source)
XLA Modules:
  0.0 134.0 jit_solution(5485729146315143049)
XLA Ops:
  7.2 0.0 all-gather.2.cloned.1.call-start
  7.2 1.8 %constant_dynamic-slice_fusion.4 = bf16[16,32,2,1,128]{4,3,2,1,0:T(2,128)(2,1)S(1)} fusion(bf16[16,128,2,4,128]{4,3,2,1,0:T(4,128)(2,1)} %param.24, s32[]{:T(128)S(6)} %select_n.11, s32[]{:T(128)S(6)} %select_n.12), kind=kLoop, calls=%fused_computation.10 | loop fusion | bytes 524296 | tf_op jit(solution)/shard_map/dynamic_slice | solution.py:414
  9.1 0.8 copy.39
  9.8 0.0 all-gather.2.cloned.1.call-update
  9.9 0.0 copy-start.17
  9.9 0.0 copy-start.18
  9.9 0.0 copy-start.15
  9.9 0.0 copy-start.16
  9.9 2.3 %cut_states.1 = bf16[16,4,32,256]{3,2,1,0:T(8,128)(2,1)} custom-call(bf16[4,16,32,256]{3,2,1,0:T(8,128)(2,1)} %bitcast.41), custom_call_target="tpu_custom_call" | custom-call | bytes 2097152 | tf_op jit(solution)/shard_map/cut_states/pallas_call | solution.py:348
  12.2 8.6 %all-to-all-start = ((bf16[16,4,32,256]{3,2,1,0:T(8,128)(2,1)}), bf16[16,4,32,256]{3,2,1,0:T(8,128)(2,1)}, u32[]{:S(2)}, u32[]{:S(2)}) async-start(bf16[16,4,32,256]{3,2,1,0:T(8,128)(2,1)} %cut_states.1), calls=%async_computation | async-start | bytes 2097152 | tf_op jit(solution)/shard_map/all_to_all | solution.py:421
  20.9 0.0 copy-done.17
  20.9 0.1 copy.38.decay_ref
  21.0 0.0 copy-done.18
  21.0 0.1 broadcast_in_dim.10
  21.1 0.1 broadcast_in_dim_reshape.3.skip_ref
  21.1 0.0 copy-done.15
  21.1 0.1 copy.31
  21.2 0.7 reshape.41.po_ref
  21.9 0.0 copy-done.16
  21.9 0.1 copy.32
  22.0 0.7 reshape.42.ps_ref
  22.6 4.4 %constant_dynamic-slice_fusion.2 = (bf16[1024,1,1,256]{3,2,1,0:T(2,128)(2,1)S(1)}, bf16[1024,1,1,256]{3,2,1,0:T(2,128)(2,1)S(1)}) fusion(bf16[1024,2,4,256]{3,2,1,0:T(4,128)(2,1)} %param.20, s32[]{:T(128)S(6)} %select_n.12, s32[]{:T(128)S(6)} %add.18), kind=kLoop, calls=%fused_computation.8 | loop fusion | bytes 2097160 | tf_op jit(solution)/shard_map/slice | solution.py:428
  27.1 0.0 copy-start.14
  27.1 0.1 copy.54
  27.2 0.1 copy.55
  27.3 1.4 %constant_dynamic-slice_fusion.3 = (bf16[256,1,1,128]{3,2,1,0:T(2,128)(2,1)S(1)}, bf16[256,1,1,128]{3,2,1,0:T(2,128)(2,1)S(1)}) fusion(bf16[1024,2,4,128]{3,2,1,0:T(4,128)(2,1)} %param.22, s32[]{:T(128)S(6)} %select_n.13, s32[]{:T(128)S(6)} %add.18, s32[]{:T(128)S(6)} %select_n.12), kind=kLoop, calls=%fused_computation.9 | loop fusion | bytes 262156 | tf_op jit(solution)/shard_map/slice | solution.py:451
  28.7 0.1 copy-done.14
  28.8 3.0 %fusion = (bf16[1024,1,512]{2,1,0:T(2,128)(2,1)S(1)}, bf16[1024,1,512]{2,1,0:T(2,128)(2,1)S(1)}) fusion(bf16[1024,2,512]{2,1,0:T(2,128)(2,1)S(1)} %copy-done.14), kind=kLoop, calls=%fused_computation.11 | loop fusion | bytes 4194304 | tf_op jit(solution)/shard_map/slice | solution.py:426
  31.8 0.0 copy-start.2
  31.8 0.6 copy_bitcast_fusion
  32.4 23.6 %all-to-all-done = bf16[16,4,32,256]{3,2,1,0:T(8,128)(2,1)} async-done(((bf16[16,4,32,256]{3,2,1,0:T(8,128)(2,1)}), bf16[16,4,32,256]{3,2,1,0:T(8,128)(2,1)}, u32[]{:S(2)}, u32[]{:S(2)}) %all-to-all-start) | async-done | bytes 1048608 | tf_op jit(solution)/shard_map/all_to_all | solution.py:421
  56.0 4.5 %all-to-all-start.1 = ((bf16[4,256,256]{2,1,0:T(8,128)(2,1)}), bf16[4,256,256]{2,1,0:T(8,128)(2,1)}, u32[]{:S(2)}, u32[]{:S(2)}) async-start(bf16[4,256,256]{2,1,0:T(8,128)(2,1)} %bitcast.42), calls=%async_computation.1 | async-start | bytes 1048576 | tf_op jit(solution)/shard_map/all_to_all | solution.py:423
  60.5 0.0 copy-done.2
  60.5 8.8 %mixer_local.1 = (f32[1024,512]{1,0:T(8,128)S(1)}, f32[1024,512]{1,0:T(8,128)S(1)}, f32[4,512,256]{2,1,0:T(8,128)S(1)}, f32[4,512,128]{2,1,0:T(8,128)S(1)}) custom-call(bf16[1024,512]{1,0:T(8,128)(2,1)S(1)} %get-tuple-element.27.x_ref, bf16[1024,512]{1,0:T(8,128)(2,1)S(1)} %get-tuple-element.26.z_ref, f32[8,1024]{1,0:T(8,128)S(1)} %bitcast.38, ...), custom_call_target="tpu_custom_call" | custom-call | flops 2000000000 | bytes 11534336 | tf_op jit(solution)/shard_map/mixer_local/pallas_call | solution.py:104
  69.3 0.0 copy-start.6
  69.3 1.4 %copy-done.6 = f32[1024,512]{1,0:T(8,128)} copy-done((f32[1024,512]{1,0:T(8,128)}, f32[1024,512]{1,0:T(8,128)S(1)}, u32[]{:S(2)}) %copy-start.6) | copy-done | bytes 2097176
  70.7 0.0 copy-start.8
  70.7 1.4 %copy-done.8 = f32[1024,512]{1,0:T(8,128)} copy-done((f32[1024,512]{1,0:T(8,128)}, f32[1024,512]{1,0:T(8,128)S(1)}, u32[]{:S(2)}) %copy-start.8) | copy-done | bytes 2097176
  72.1 0.0 copy-start.10
  72.1 1.4 %copy-done.10 = f32[4,512,256]{2,1,0:T(8,128)} copy-done((f32[4,512,256]{2,1,0:T(8,128)}, f32[4,512,256]{2,1,0:T(8,128)S(1)}, u32[]{:S(2)}) %copy-start.10) | copy-done | bytes 2097176
  73.5 0.0 copy-start.12
  73.5 1.0 copy-done.12
  74.5 0.0 all-gather.2.cloned.1.call-done.pool_ref
  74.5 0.0 copy-start.3
  74.5 0.0 copy-start.4
  74.5 0.0 copy-start.5
  74.6 0.0 copy-start.13
  74.6 3.9 %pick.1 = (bf16[64,32,256]{2,1,0:T(8,128)(2,1)}, bf16[64,64,128]{2,1,0:T(8,128)(2,1)}) custom-call(s32[64]{0:T(128)} %bitcast.43, s32[64]{0:T(128)} %hs_ref.1, s32[1024]{0:T(1024)} %reshape.41.po_ref, s32[1024]{0:T(1024)} %reshape.42.ps_ref, s32[1]{0:T(128)} %bitcast.1.base_ref, bf16[64,32,256]{2,1,0:T(8,128)(2,1)} %bitcast.3.hop_ref, ...), custom_call_target="tpu_custom_call" | custom-call | bytes 4194304 | tf_op jit(solution)/shard_map/pick/pallas_call | solution.py:377
  78.5 0.0 all-to-all-done.1.q_ref
  78.5 0.0 copy-done.3
  78.5 0.0 copy-done.4
  78.5 0.0 copy-done.5
  78.5 0.0 copy-done.13
  78.5 0.0 copy-start
  78.5 1.2 copy-done
  79.7 0.0 copy-start.1
  79.7 1.2 copy-done.1
  81.0 0.0 copy-start.7
  81.0 1.6 %copy-done.7 = f32[1024,512]{1,0:T(8,128)S(1)} copy-done((f32[1024,512]{1,0:T(8,128)S(1)}, f32[1024,512]{1,0:T(8,128)}, u32[]{:S(2)}) %copy-start.7) | copy-done | bytes 2097176
  82.6 1.6 %copy-done.9 = f32[1024,512]{1,0:T(8,128)S(1)} copy-done((f32[1024,512]{1,0:T(8,128)S(1)}, f32[1024,512]{1,0:T(8,128)}, u32[]{:S(2)}) %copy-start.9) | copy-done | bytes 2097176
  84.1 1.6 %copy-done.11 = f32[4,512,256]{2,1,0:T(8,128)S(1)} copy-done((f32[4,512,256]{2,1,0:T(8,128)S(1)}, f32[4,512,256]{2,1,0:T(8,128)}, u32[]{:S(2)}) %copy-start.11) | copy-done | bytes 2097176
  85.7 39.6 %finish.1 = (bf16[1024,512]{1,0:T(8,128)(2,1)S(1)}, bf16[4,256,256]{2,1,0:T(8,128)(2,1)S(1)}) custom-call(s32[64]{0:T(128)S(1)} %copy-done.4, s32[64]{0:T(128)S(1)} %copy-done.5, bf16[16,4,32,256]{3,2,1,0:T(8,128)(2,1)S(1)} %bitcast.36, bf16[4,16,64,128]{3,2,1,0:T(8,128)(2,1)S(1)} %bitcast.37, bf16[4,256,256]{2,1,0:T(8,128)(2,1)} %all-to-all-done.1.q_ref, ...), custom_call_target="tpu_custom_call" | custom-call | flops 3000000000 | bytes 16777216 | tf_op jit(solution)/shard_map/finish/pallas_call | solution.py:309
  125.4 1.0 copy.58
  126.4 0.8 copy.59
  (3 shorter events, 0.0 us)
Async XLA Ops:
  7.2 67.4 %all-gather.2.cloned.1.call-start = ((), (), s32[]{:S(2)}) async-start(), calls=%async_computation.2 | async-start | bytes 4456448 | tf_op jit(solution)/shard_map/all_gather | solution.py:418
  9.9 11.0 %copy-start.17 = (f32[8]{0:T(128)S(1)}, f32[8]{0:T(128)}, u32[]{:S(2)}) copy-start(f32[8]{0:T(128)} %param.18) | copy-start | bytes 100
  9.9 11.1 %copy-start.18 = (f32[8]{0:T(128)S(1)}, f32[8]{0:T(128)}, u32[]{:S(2)}) copy-start(f32[8]{0:T(128)} %param.19) | copy-start | bytes 100
  9.9 11.3 %copy-start.15 = (s32[64,16,1]{0,2,1:T(1,128)S(1)}, s32[64,16,1]{0,2,1:T(1,128)}, u32[]{:S(2)}) copy-start(s32[64,16,1]{0,2,1:T(1,128)} %param.28) | copy-start | bytes 12292
  9.9 12.0 %copy-start.16 = (s32[64,16]{0,1:T(8,128)S(1)}, s32[64,16]{0,1:T(8,128)}, u32[]{:S(2)}) copy-start(s32[64,16]{0,1:T(8,128)} %param.29) | copy-start | bytes 12292
  12.2 43.8 %all-to-all-start = ((bf16[16,4,32,256]{3,2,1,0:T(8,128)(2,1)}), bf16[16,4,32,256]{3,2,1,0:T(8,128)(2,1)}, u32[]{:S(2)}, u32[]{:S(2)}) async-start(bf16[16,4,32,256]{3,2,1,0:T(8,128)(2,1)} %cut_states.1), calls=%async_computation | async-start | bytes 2097152 | tf_op jit(solution)/shard_map/all_to_all | solution.py:421
  27.1 1.8 %copy-start.14 = (bf16[1024,2,512]{2,1,0:T(2,128)(2,1)S(1)}, bf16[1024,2,512]{2,1,0:T(2,128)(2,1)}, u32[]{:S(2)}) copy-start(bf16[1024,2,512]{2,1,0:T(2,128)(2,1)} %param.16) | copy-start | bytes 6291460
  31.8 28.7 %copy-start.2 = (f32[1024,8]{0,1:T(8,128)S(1)}, f32[1024,8]{0,1:T(8,128)}, u32[]{:S(2)}) copy-start(f32[1024,8]{0,1:T(8,128)} %param.17) | copy-start | bytes 98308
  56.0 22.4 %all-to-all-start.1 = ((bf16[4,256,256]{2,1,0:T(8,128)(2,1)}), bf16[4,256,256]{2,1,0:T(8,128)(2,1)}, u32[]{:S(2)}, u32[]{:S(2)}) async-start(bf16[4,256,256]{2,1,0:T(8,128)(2,1)} %bitcast.42), calls=%async_computation.1 | async-start | bytes 1048576 | tf_op jit(solution)/shard_map/all_to_all | solution.py:423
  69.3 1.4 %copy-start.6 = (f32[1024,512]{1,0:T(8,128)}, f32[1024,512]{1,0:T(8,128)S(1)}, u32[]{:S(2)}) copy-start(f32[1024,512]{1,0:T(8,128)S(1)} %get-tuple-element.12.p_ref) | copy-start | bytes 6291460
  70.7 1.4 %copy-start.8 = (f32[1024,512]{1,0:T(8,128)}, f32[1024,512]{1,0:T(8,128)S(1)}, u32[]{:S(2)}) copy-start(f32[1024,512]{1,0:T(8,128)S(1)} %get-tuple-element.13.e_ref) | copy-start | bytes 6291460
  72.1 1.4 %copy-start.10 = (f32[4,512,256]{2,1,0:T(8,128)}, f32[4,512,256]{2,1,0:T(8,128)S(1)}, u32[]{:S(2)}) copy-start(f32[4,512,256]{2,1,0:T(8,128)S(1)} %get-tuple-element.14.bs_ref) | copy-start | bytes 6291460
  73.5 1.0 copy-start.12
  74.5 3.9 %copy-start.3 = (f32[512]{0:T(512)S(1)}, f32[512]{0:T(512)}, u32[]{:S(2)}) copy-start(f32[512]{0:T(512)} %param.25) | copy-start | bytes 6148
  74.5 3.9 %copy-start.4 = (s32[64]{0:T(128)S(1)}, s32[64]{0:T(128)}, u32[]{:S(2)}) copy-start(s32[64]{0:T(128)} %pre_ref.1) | copy-start | bytes 772
  74.5 3.9 %copy-start.5 = (s32[64]{0:T(128)S(1)}, s32[64]{0:T(128)}, u32[]{:S(2)}) copy-start(s32[64]{0:T(128)} %suf_ref.1) | copy-start | bytes 772
  74.6 3.9 %copy-start.13 = (f32[4,512,128]{2,1,0:T(8,128)S(1)}, f32[4,512,128]{2,1,0:T(8,128)}, u32[]{:S(2)}) copy-start(f32[4,512,128]{2,1,0:T(8,128)} %copy-done.12) | copy-start | bytes 3145732
  78.5 1.2 copy-start
  79.7 1.2 copy-start.1
  81.0 1.6 %copy-start.7 = (f32[1024,512]{1,0:T(8,128)S(1)}, f32[1024,512]{1,0:T(8,128)}, u32[]{:S(2)}) copy-start(f32[1024,512]{1,0:T(8,128)} %copy-done.6) | copy-start | bytes 6291460
  82.6 1.6 %copy-start.9 = (f32[1024,512]{1,0:T(8,128)S(1)}, f32[1024,512]{1,0:T(8,128)}, u32[]{:S(2)}) copy-start(f32[1024,512]{1,0:T(8,128)} %copy-done.8) | copy-start | bytes 6291460
  84.1 1.6 %copy-start.11 = (f32[4,512,256]{2,1,0:T(8,128)S(1)}, f32[4,512,256]{2,1,0:T(8,128)}, u32[]{:S(2)}) copy-start(f32[4,512,256]{2,1,0:T(8,128)} %copy-done.10) | copy-start | bytes 6291460
Sparse Core Ops, SparseCore 0:
  10.4 62.1 all-gather.1

commit v3 on v2

v3 whole, which is shorter than its diff:
```python
import functools
import math

import jax
import jax.numpy as jnp
from jax import lax
from jax.experimental import pallas as pl
from jax.experimental.pallas import tpu as pltpu
from jax.sharding import Mesh
from jax.sharding import PartitionSpec as P

HEADS = 8
MHDIM = 64
CH = HEADS * MHDIM
STATE = 256
GROUP_CH = 2048
HD = 128
PAGE = 128
SPAN = 128
SUF = 256
MAXP = 16
REQ = 4
QUARTER = PAGE // 4
EPSILON = 1e-05
NEG = -1e30
OWN = ("z", "core")
BF = jnp.bfloat16
F32 = jnp.float32
HI = lax.Precision.HIGHEST


def dot_nt(a, b):
    return lax.dot_general(a, b, (((1,), (1,)), ((), ())), preferred_element_type=F32)


def dot_nn(a, b):
    return lax.dot_general(a, b, (((1,), (0,)), ((), ())), preferred_element_type=F32)


def dot_tn(a, b):
    return lax.dot_general(a, b, (((0,), (0,)), ((), ())), preferred_element_type=F32)


def expand(cols):
    head = lax.broadcasted_iota(jnp.int32, (HEADS, CH), 0)
    chan = lax.broadcasted_iota(jnp.int32, (HEADS, CH), 1)
    pick = (chan // MHDIM == head).astype(F32)
    return lax.dot_general(
        cols, pick, (((1,), (0,)), ((), ())), preferred_element_type=F32, precision=HI
    )


MESH = pl.DeviceIdType.MESH


def attend_pair(q_ref, k, v, ks, vs, bias, causal, live, o_ref, slot):
    scale = 1.0 / math.sqrt(HD)
    for half in range(2):
        lanes = pl.ds(half * HD, HD)
        q = q_ref[slot, :, lanes]
        s_pre = dot_nt(q, k) * scale + bias
        s_suf = jnp.where(causal, dot_nt(q, ks) * scale, NEG)
        top = jnp.maximum(
            jnp.max(s_pre, axis=1, keepdims=True), jnp.max(s_suf, axis=1, keepdims=True)
        )
        w_pre = jnp.exp(s_pre - top)
        w_suf = jnp.exp(s_suf - top)
        total = jnp.sum(w_pre, axis=1, keepdims=True) + jnp.sum(w_suf, axis=1, keepdims=True)
        mixed = dot_nn(w_pre.astype(BF), v) + dot_nn(w_suf.astype(BF), vs)
        o_ref[slot, :, lanes] = jnp.where(live, mixed / total, 0.0).astype(BF)


def program_kernel(
    ho_ref,
    hs_ref,
    po_ref,
    ps_ref,
    pre_ref,
    suf_ref,
    decay_ref,
    skip_ref,
    mix_hbm,
    step_hbm,
    proj_hbm,
    query_hbm,
    suffix_hbm,
    state_hbm,
    page_hbm,
    gain_hbm,
    mamba_ref,
    attn_ref,
    mix_raw,
    step_buf,
    proj_raw,
    suf_raw,
    page_raw,
    gain_buf,
    q_buf,
    b_buf,
    c_buf,
    ks_buf,
    vs_buf,
    p_buf,
    e_buf,
    bs_buf,
    dec_buf,
    pool_buf,
    hop_buf,
    want_buf,
    mine_buf,
    st_buf,
    kv_buf,
    o_buf,
    sum_buf,
    load_sem,
    q_send,
    q_recv,
    hop_send,
    hop_recv,
    st_send,
    st_recv,
    right_send,
    right_recv,
    left_send,
    left_recv,
    sib_send,
    sib_recv,
    kv_send,
    kv_recv,
    o_send,
    o_recv,
    sum_send,
    sum_recv,
):
    x = lax.axis_index("x")
    y = lax.axis_index("y")
    z = lax.axis_index("z")
    core = lax.axis_index("core")
    me = z * 2 + core
    barrier = pltpu.get_barrier_semaphore()

    def owner_id(k):
        other = lax.rem(me + k, 16)
        return other, {"z": other // 2, "core": lax.rem(other, 2)}

    def y_id(k):
        other = lax.rem(y + k, 4)
        return other, {"y": other}

    def send(src, dst, send_sem, recv_sem, device):
        return pltpu.make_async_remote_copy(
            src, dst, send_sem, recv_sem, device_id=device, device_id_type=MESH
        )

    def q_copy(k):
        other, device = y_id(k)
        return send(query_hbm.at[other], q_buf.at[y], q_send.at[k], q_recv.at[k], device)

    def hop_copy(k):
        other, device = owner_id(k)
        return send(state_hbm.at[:, other], hop_buf.at[me], hop_send.at[k], hop_recv.at[k], device)

    def state_copy(k):
        other, device = owner_id(k)
        return send(want_buf.at[other], st_buf.at[me], st_send.at[k], st_recv.at[k], device)

    def right_copy(s):
        piece = lax.rem(z - s + 9, 8) * 2 + core
        ref = pool_buf.at[piece]
        return send(ref, ref, right_send.at[s], right_recv.at[s], {"z": lax.rem(z + 1, 8)})

    def left_copy(s):
        piece = lax.rem(z + s - 1, 8) * 2 + core
        ref = pool_buf.at[piece]
        return send(ref, ref, left_send.at[s], left_recv.at[s], {"z": lax.rem(z + 7, 8)})

    def right_last():
        piece = lax.rem(z + 5, 8) * 2 + core
        ref = pool_buf.at[piece, pl.ds(0, 8)]
        return send(ref, ref, right_send.at[4], right_recv.at[4], {"z": lax.rem(z + 1, 8)})

    def left_last():
        piece = lax.rem(z + 3, 8) * 2 + core
        ref = pool_buf.at[piece, pl.ds(8, 8)]
        return send(ref, ref, left_send.at[4], left_recv.at[4], {"z": lax.rem(z + 7, 8)})

    def sibling_copy(far, k):
        piece = lax.rem(z + far, 8) * 2 + core
        ref = pool_buf.at[piece]
        return send(ref, ref, sib_send.at[k], sib_recv.at[k], {"core": 1 - core})

    def page_copy(k):
        other, device = y_id(k)
        return send(mine_buf.at[other], kv_buf.at[y], kv_send.at[k], kv_recv.at[k], device)

    def out_copy(k):
        other, device = y_id(k)
        return send(o_buf.at[other], attn_ref.at[y], o_send.at[k], o_recv.at[k], device)

    def sum_copy(k):
        device = y_id(k)[1]
        return send(sum_buf.at[y], sum_buf.at[y], sum_send.at[k], sum_recv.at[k], device)

    load_pages = pltpu.make_async_copy(page_hbm.at[:, pl.ds(y * QUARTER, QUARTER)], page_raw, load_sem.at[0])
    load_proj = pltpu.make_async_copy(proj_hbm, proj_raw, load_sem.at[1])
    load_mix = pltpu.make_async_copy(mix_hbm, mix_raw, load_sem.at[2])
    load_step = pltpu.make_async_copy(step_hbm, step_buf, load_sem.at[3])
    load_suf = pltpu.make_async_copy(suffix_hbm.at[pl.ds(y * SUF, SUF)], suf_raw, load_sem.at[4])
    load_gain = pltpu.make_async_copy(gain_hbm, gain_buf, load_sem.at[5])
    load_q = pltpu.make_async_copy(query_hbm.at[y], q_buf.at[y], load_sem.at[6])
    load_hop = pltpu.make_async_copy(state_hbm.at[:, me], hop_buf.at[me], load_sem.at[7])
    load_pages.start()

    def greet(k, carry):
        pl.semaphore_signal(barrier, inc=1, device_id=owner_id(k)[1], device_id_type=MESH)
        return carry

    lax.fori_loop(1, 16, greet, 0)
    for k in range(1, 4):
        pl.semaphore_signal(barrier, inc=1, device_id=y_id(k)[1], device_id_type=MESH)
    for load in (load_proj, load_mix, load_step, load_suf, load_gain, load_q, load_hop):
        load.start()
    load_pages.wait()
    for head in range(4):

        @pl.when(x == head)
        def _(head=head):
            def extract(i, carry):
                pool_buf[me, i, 0:QUARTER, :] = page_raw[i, :, 0, head, :]
                pool_buf[me, i, QUARTER : 2 * QUARTER, :] = page_raw[i, :, 1, head, :]
                return carry

            lax.fori_loop(0, 16, extract, 0)

    pl.semaphore_wait(barrier, 18)
    right_copy(1).start()
    left_copy(1).start()
    sibling_copy(0, 0).start()

    def send_hop(k, carry):
        hop_copy(k).start()
        return carry

    lax.fori_loop(1, 16, send_hop, 0)
    for k in (2, 1, 3):
        q_copy(k).start()

    load_proj.wait()
    load_suf.wait()
    for head in range(4):

        @pl.when(x == head)
        def _(head=head):
            def extract(i, carry):
                rows = pl.ds(pl.multiple_of(i * 64, 64), 64)
                b_buf[rows, :] = proj_raw[rows, 0, head, :]
                c_buf[rows, :] = proj_raw[rows, 1, head, :]
                return carry

            lax.fori_loop(0, 16, extract, 0)
            ks_buf[...] = suf_raw[:, 0, head, :]
            vs_buf[...] = suf_raw[:, 1, head, :]

    load_mix.wait()
    load_step.wait()

    def mixer_local(j):
        lane = lax.broadcasted_iota(jnp.int32, (HEADS, SPAN), 1)
        head_row = lax.broadcasted_iota(jnp.int32, (HEADS, SPAN), 0)
        lower = lax.broadcasted_iota(jnp.int32, (SPAN, SPAN), 0) >= lax.broadcasted_iota(
            jnp.int32, (SPAN, SPAN), 1
        )
        low_half = lax.broadcasted_iota(jnp.int32, (SPAN, 2 * MHDIM), 1) < MHDIM
        decay = jnp.zeros((HEADS, SPAN), F32)
        for h in range(HEADS):
            decay = jnp.where(head_row == h, decay_ref[h], decay)
        for blk in range(SUF // SPAN):
            rows = pl.ds(pl.multiple_of(j * SUF + blk * SPAN, SPAN), SPAN)
            raw = step_buf[:, rows]
            rate = jnp.maximum(raw, 0.0) + jnp.log(1.0 + jnp.exp(-jnp.abs(raw)))
            cum = -rate * decay
            shift = 1
            while shift < SPAN:
                cum = cum + jnp.where(lane >= shift, pltpu.roll(cum, shift, 1), 0.0)
                shift *= 2
            cum_col = jnp.transpose(cum)
            xs = mix_raw[rows, 0, :]
            zs = mix_raw[rows, 1, :]
            b = b_buf[rows, :]
            inter = dot_nt(c_buf[rows, :], b)
            for pair in range(HEADS // 2):
                parts = []
                for h in (2 * pair, 2 * pair + 1):
                    gap = cum_col[:, h : h + 1] - cum[h : h + 1, :]
                    fade = jnp.exp(jnp.where(lower, gap, NEG))
                    parts.append((inter * fade * rate[h : h + 1, :]).astype(BF))
                lanes = slice(pair * 2 * MHDIM, (pair + 1) * 2 * MHDIM)
                xp = xs[:, lanes]
                inner = jnp.where(low_half, dot_nn(parts[0], xp), dot_nn(parts[1], xp))
                zp = zs[:, lanes].astype(F32)
                gate = zp / (1.0 + jnp.exp(-zp))
                skip = jnp.where(low_half, skip_ref[2 * pair], skip_ref[2 * pair + 1])
                p_buf[rows, lanes] = (inner + skip * xp.astype(F32)) * gate
                grow = jnp.where(
                    low_half,
                    jnp.broadcast_to(cum_col[:, 2 * pair : 2 * pair + 1], (SPAN, 2 * MHDIM)),
                    jnp.broadcast_to(cum_col[:, 2 * pair + 1 : 2 * pair + 2], (SPAN, 2 * MHDIM)),
                )
                e_buf[rows, lanes] = jnp.exp(grow) * gate
            if blk == 0:
                end = cum[:, SPAN - 1 : SPAN]
                tail = jnp.transpose(jnp.exp(end - cum) * rate)
                scaled = (expand(tail) * xs.astype(F32)).astype(BF)
                bs_buf[j] = dot_tn(scaled, b)
                keep = jnp.transpose(jnp.broadcast_to(jnp.exp(end), (HEADS, SPAN)))
                dec_buf[j] = jnp.transpose(expand(keep))

    def ring_step(s, carry):
        mixer_local(s - 1)
        right_copy(s).wait()
        left_copy(s).wait()

        @pl.when(s < 3)
        def _():
            right_copy(s + 1).start()
            left_copy(s + 1).start()

        @pl.when(s == 3)
        def _():
            right_last().start()
            left_last().start()

        sibling_copy(8 - s, 2 * s - 1).start()
        sibling_copy(s, 2 * s).start()
        return carry

    lax.fori_loop(1, 4, ring_step, 0)
    mixer_local(3)
    right_last().wait()
    left_last().wait()
    sibling_copy(4, 7).start()

    def wait_hop(k, carry):
        hop_copy(k).wait()
        return carry

    lax.fori_loop(1, 16, wait_hop, 0)
    load_hop.wait()

    def pick_state(i, carry):
        want_buf[i // REQ, lax.rem(i, REQ)] = hop_buf[ho_ref[i], hs_ref[i]]
        return carry

    lax.fori_loop(0, 64, pick_state, 0)

    def send_state(k, carry):
        state_copy(k).start()
        return carry

    lax.fori_loop(1, 16, send_state, 0)
    st_buf[me] = want_buf[me]

    def wait_sibling(k, carry):
        sibling_copy(0, k).wait()
        return carry

    lax.fori_loop(0, 8, wait_sibling, 0)

    def pick_page(i, carry):
        r = i // MAXP
        p = lax.rem(i, MAXP)
        mine_buf[r, p] = pool_buf[po_ref[p, me * REQ + r], ps_ref[p, me * REQ + r]]
        return carry

    lax.fori_loop(0, 64, pick_page, 0)
    for k in (2, 1, 3):
        page_copy(k).start()
    kv_buf[y] = mine_buf[y]
    for k in (1, 2, 3):
        q_copy(k).wait()
    load_q.wait()
    for k in (1, 2, 3):
        page_copy(k).wait()

    request = me * REQ + y
    keys = MAXP * PAGE
    page = (lax.broadcasted_iota(jnp.int32, (1, keys), 1) // QUARTER) % MAXP
    bias = jnp.where(page * PAGE < pre_ref[request], 0.0, NEG)
    causal = lax.broadcasted_iota(jnp.int32, (SUF, SUF), 0) >= lax.broadcasted_iota(jnp.int32, (SUF, SUF), 1)
    live = lax.broadcasted_iota(jnp.int32, (SUF, HD), 0) < suf_ref[request]

    def attend_step(t, carry):
        kv = kv_buf[...].reshape(4 * MAXP, 2 * QUARTER, HD)
        k = kv[:, :QUARTER, :].reshape(keys, HD)
        v = kv[:, QUARTER:, :].reshape(keys, HD)
        slot = lax.rem(y + t, 4)
        attend_pair(q_buf, k, v, ks_buf[...], vs_buf[...], bias, causal, live, o_buf, slot)

        @pl.when(t < 4)
        def _():
            out_copy(t).start()

        return carry

    lax.fori_loop(1, 5, attend_step, 0)
    attn_ref[y] = o_buf[y]

    def wait_state(k, carry):
        state_copy(k).wait()
        return carry

    lax.fori_loop(1, 16, wait_state, 0)

    def mixer_step(j, carry):
        start = st_buf[:, j].reshape(CH, STATE)
        dec = dec_buf[j]
        begin = jnp.concatenate([dec, dec], axis=1) * start.astype(F32) + bs_buf[j]
        for blk, state in enumerate((start, begin.astype(BF))):
            rows = pl.ds(pl.multiple_of(j * SUF + blk * SPAN, SPAN), SPAN)
            carried = dot_nt(c_buf[rows, :], state)
            gated = p_buf[rows, :] + e_buf[rows, :] * carried
            p_buf[rows, :] = gated
            total = jnp.sum(gated * gated, axis=1, keepdims=True)
            sum_buf[y, pl.ds(2 * j + blk, 1), :] = jnp.transpose(jnp.broadcast_to(total, (SPAN, SPAN)))[0:1, :]
        return carry

    lax.fori_loop(0, REQ, mixer_step, 0)
    for k in (2, 1, 3):
        sum_copy(k).start()
    load_gain.wait()
    for k in (1, 2, 3):
        sum_copy(k).wait()

    def norm_step(i, carry):
        rows = pl.ds(pl.multiple_of(i * SPAN, SPAN), SPAN)
        square = jnp.sum(sum_buf[:, pl.ds(i, 1), :], axis=0) / GROUP_CH
        factor = jnp.transpose(jnp.broadcast_to(lax.rsqrt(square + EPSILON), (SPAN, SPAN)))
        token = lax.broadcasted_iota(jnp.int32, (SPAN, SPAN), 0) + lax.rem(i, 2) * SPAN
        alive = token < suf_ref[me * REQ + i // 2]
        for part in range(CH // SPAN):
            lanes = pl.ds(part * SPAN, SPAN)
            value = p_buf[rows, lanes] * factor * gain_buf[:, lanes]
            mamba_ref[rows, lanes] = jnp.where(alive, value, 0.0).astype(BF)
        return carry

    lax.fori_loop(0, 8, norm_step, 0)
    for k in (1, 2, 3):
        out_copy(k).wait()


def run_program(scalars, arrays):
    vmem = pl.BlockSpec(memory_space=pltpu.VMEM)
    smem = pl.BlockSpec(memory_space=pltpu.SMEM)
    hbm = pl.BlockSpec(memory_space=pltpu.HBM)
    dma = pltpu.SemaphoreType.DMA
    tok = REQ * SUF
    return pl.pallas_call(
        program_kernel,
        in_specs=[smem] * len(scalars) + [hbm] * len(arrays),
        out_specs=[vmem, vmem],
        out_shape=[
            jax.ShapeDtypeStruct((tok, CH), BF),
            jax.ShapeDtypeStruct((4, SUF, 2 * HD), BF),
        ],
        scratch_shapes=[
            pltpu.VMEM((tok, 2, CH), BF),
            pltpu.VMEM((HEADS, tok), F32),
            pltpu.VMEM((tok, 2, 4, STATE), BF),
            pltpu.VMEM((SUF, 2, 4, HD), BF),
            pltpu.VMEM((16, QUARTER, 2, 4, HD), BF),
            pltpu.VMEM((1, CH), F32),
            pltpu.VMEM((4, SUF, 2 * HD), BF),
            pltpu.VMEM((tok, STATE), BF),
            pltpu.VMEM((tok, STATE), BF),
            pltpu.VMEM((SUF, HD), BF),
            pltpu.VMEM((SUF, HD), BF),
            pltpu.VMEM((tok, CH), F32),
            pltpu.VMEM((tok, CH), F32),
            pltpu.VMEM((REQ, CH, STATE), F32),
            pltpu.VMEM((REQ, CH, SPAN), F32),
            pltpu.VMEM((16, 16, 2 * QUARTER, HD), BF),
            pltpu.VMEM((16, 4, CH // 16, STATE), BF),
            pltpu.VMEM((16, REQ, CH // 16, STATE), BF),
            pltpu.VMEM((REQ, MAXP, 2 * QUARTER, HD), BF),
            pltpu.VMEM((16, REQ, CH // 16, STATE), BF),
            pltpu.VMEM((4, MAXP, 2 * QUARTER, HD), BF),
            pltpu.VMEM((4, SUF, 2 * HD), BF),
            pltpu.VMEM((4, 8, SPAN), F32),
            dma((8,)),
            dma((4,)),
            dma((4,)),
            dma((16,)),
            dma((16,)),
            dma((16,)),
            dma((16,)),
            dma((5,)),
            dma((5,)),
            dma((5,)),
            dma((5,)),
            dma((8,)),
            dma((8,)),
            dma((4,)),
            dma((4,)),
            dma((4,)),
            dma((4,)),
            dma((4,)),
            dma((4,)),
        ],
        compiler_params=pltpu.CompilerParams(
            collective_id=0, has_side_effects=True, vmem_limit_bytes=56 << 20
        ),
        cost_estimate=pl.CostEstimate(flops=5_000_000_000, bytes_accessed=16 << 20, transcendentals=8 << 20),
        name="prefill",
    )(*scalars, *arrays)


def body(
    mixer_input,
    step_raw,
    decay_rate,
    skip_gain,
    state_proj,
    queries,
    suffix_kv,
    state_pool,
    page_pool,
    norm_gain,
    hit_owner,
    hit_slot,
    page_owner,
    page_slot,
    prefix_len,
    suffix_len,
):
    scalars = (
        hit_owner.reshape(-1),
        hit_slot,
        page_owner[:, :, 0].T,
        page_slot.T,
        prefix_len,
        suffix_len,
        decay_rate,
        skip_gain,
    )
    arrays = (
        mixer_input,
        step_raw.T,
        state_proj,
        queries.reshape(REQ, SUF, 2 * HD),
        suffix_kv,
        state_pool.reshape(4, 16, CH // 16, STATE),
        page_pool,
        norm_gain[None],
    )
    mamba_out, attn = run_program(scalars, arrays)
    return (mamba_out, attn.reshape(REQ * SUF, 2 * HD))


def solution(mesh):
    grid = Mesh(mesh.devices.reshape(8, 2, 4, 4), ("z", "core", "x", "y"))
    col = ("x", "y")
    return jax.shard_map(
        body,
        mesh=grid,
        in_specs=(
            P(OWN, None, col),
            P(OWN, col),
            P(col),
            P(col),
            P(OWN, None, None, None),
            P(OWN, col),
            P(OWN, None, None, None),
            P(OWN, col, None, None),
            P(OWN, None, None, None, None),
            P(col),
            P(),
            P(),
            P(),
            P(),
            P(),
            P(),
        ),
        out_specs=(P(OWN, col), P(OWN, col)),
        check_vma=False,
    )
```

time: 135 us -> 96.5 us (0.71)
  Pallas kernels: 54.7 us -> 91.5 us
  local copies, waits for them, and re-layouts: 28.2 us -> 4.13 us
  waiting for transfers between devices: 23.6 us -> 0 us
  between operations: 14.3 us -> 0.65 us
  starting transfers between devices: 13.2 us -> 0 us
    pallas_call x4 -> x1, Pallas kernels: 54.7 us -> 91.5 us  [run_program(): pl.pallas_call(program_kernel, in_specs=[smem] * len(scalars) + [hbm] * l...]
    all_to_all x2 -> x0, waiting for transfers between devices: 23.6 us -> none  [the longest x1 23.6 us: body(): hop = lax.all_to_all(cut, OWN, split_axis=0, concat_axis=0, tiled=True)]
    all_to_all x2 -> x0, starting transfers between devices: 13.1 us -> none  [the longest x1 8.63 us: body(): hop = lax.all_to_all(cut, OWN, split_axis=0, concat_axis=0, tiled=True)]
    unnamed x45 -> x2, local copies, waits for them, and re-layouts: 15.4 us -> 4.13 us
    slice x3 -> x0, local copies, waits for them, and re-layouts: 8.81 us -> none  [the longest x1 4.42 us: body(): b = maps[:, 0, 0]]
    dynamic_slice x1 -> x0, local copies, waits for them, and re-layouts: 1.85 us -> none  [body(): lax.dynamic_slice(page_pool, (0, y_index * QUARTER, 0, x_index, 0), (16,...]
  transfers between devices with their start and end apart: 3 -> 0, of which waited for: 1 -> 0; matrix products, arithmetic and copies ran while one was open for 8% -> 0% of each run, Pallas kernels for 11% -> 0%
where the time goes in v3:
time: 96.5 us; the launch traced here: 96.3 us
  Pallas kernels  91.5 us (95%)
  local copies, waits for them, and re-layouts  4.13 us (4%)
    pallas_call x1, Pallas kernels, run_program(): pl.pallas_call(program_kernel, in_specs=[smem] * len(scalars) + [hbm] * l...  91.5 us
    unnamed x2, local copies, waits for them, and re-layouts  4.13 us

profile of v3, /device:TPU:6, one launch (start us, length us, event | category | flops | bytes accessed | tf_op | source)
XLA Modules:
  0.0 96.3 jit_solution(208750299724839673)
XLA Ops:
  0.6 91.5 %prefill.1 = (bf16[1024,512]{1,0:T(8,128)(2,1)}, bf16[4,256,256]{2,1,0:T(8,128)(2,1)}) custom-call(s32[64]{0:T(128)} %bitcast.17, s32[64]{0:T(128)} %hs_ref.1, s32[16,64]{1,0:T(8,128)} %bitcast.14, s32[16,64]{1,0:T(8,128)} %bitcast.15, s32[64]{0:T(128)} %pre_ref.1, s32[64]{0:T(128)} %suf_ref.1, f32[8]{0:T(128)} %decay_ref.1, f32[8]{0:T(128)} %skip_ref.1, ...), custom_call_target="tpu_custom_call" | custom-call | flops 5000000000 | bytes 16777216 | tf_op jit(solution)/shard_map/prefill/pallas_call | solution.py:457
  92.2 2.3 %copy.20 = bf16[1024,512]{1,0:T(8,128)(2,1)} copy(bf16[1024,512]{1,0:T(8,128)(2,1)} %get-tuple-element.8) | data formatting | bytes 2097152
  94.4 1.9 %copy.21 = bf16[1024,256]{1,0:T(8,128)(2,1)} copy(bf16[1024,256]{1,0:T(8,128)(2,1)} %bitcast.10) | data formatting | bytes 1048576

commit v4 on v3

--- a/solution.py
+++ b/solution.py
@@ -237,11 +237,14 @@
     left_copy(1).start()
     sibling_copy(0, 0).start()
 
-    def send_hop(k, carry):
-        hop_copy(k).start()
-        return carry
-
-    lax.fori_loop(1, 16, send_hop, 0)
+    def send_hops(group):
+        def send_hop(i, carry):
+            hop_copy(lax.rem(group + 1, 3) * 5 + 1 + i).start()
+            return carry
+
+        lax.fori_loop(0, 5, send_hop, 0)
+
+    send_hops(0)
     for k in (2, 1, 3):
         q_copy(k).start()
 
@@ -324,6 +327,7 @@
         def _():
             right_copy(s + 1).start()
             left_copy(s + 1).start()
+            send_hops(s)
 
         @pl.when(s == 3)
         def _():
@@ -340,26 +344,6 @@
     left_last().wait()
     sibling_copy(4, 7).start()
 
-    def wait_hop(k, carry):
-        hop_copy(k).wait()
-        return carry
-
-    lax.fori_loop(1, 16, wait_hop, 0)
-    load_hop.wait()
-
-    def pick_state(i, carry):
-        want_buf[i // REQ, lax.rem(i, REQ)] = hop_buf[ho_ref[i], hs_ref[i]]
-        return carry
-
-    lax.fori_loop(0, 64, pick_state, 0)
-
-    def send_state(k, carry):
-        state_copy(k).start()
-        return carry
-
-    lax.fori_loop(1, 16, send_state, 0)
-    st_buf[me] = want_buf[me]
-
     def wait_sibling(k, carry):
         sibling_copy(0, k).wait()
         return carry
@@ -375,6 +359,26 @@
     lax.fori_loop(0, 64, pick_page, 0)
     for k in (2, 1, 3):
         page_copy(k).start()
+    def wait_hop(k, carry):
+        hop_copy(k).wait()
+        return carry
+
+    lax.fori_loop(1, 16, wait_hop, 0)
+    load_hop.wait()
+
+    def pick_state(i, carry):
+        want_buf[i // REQ, lax.rem(i, REQ)] = hop_buf[ho_ref[i], hs_ref[i]]
+        return carry
+
+    lax.fori_loop(0, 64, pick_state, 0)
+
+    def send_state(k, carry):
+        state_copy(k).start()
+        return carry
+
+    lax.fori_loop(1, 16, send_state, 0)
+    st_buf[me] = want_buf[me]
+
     kv_buf[y] = mine_buf[y]
     for k in (1, 2, 3):
         q_copy(k).wait()

time: 96.5 us -> 100 us (1.036)
  Pallas kernels: 91.5 us -> 94.1 us
    pallas_call x1, Pallas kernels: 91.5 us -> 94.1 us  [run_program(): pl.pallas_call(program_kernel, in_specs=[smem] * len(scalars) + [hbm] * l...]
where the time goes in v4:
time: 100 us; the launch traced here: 98.9 us
  Pallas kernels  94.1 us (94%)
  local copies, waits for them, and re-layouts  4.13 us (4%)
    pallas_call x1, Pallas kernels, run_program(): pl.pallas_call(program_kernel, in_specs=[smem] * len(scalars) + [hbm] * l...  94.1 us
    unnamed x2, local copies, waits for them, and re-layouts  4.13 us

profile of v4, /device:TPU:6, one launch (start us, length us, event | category | flops | bytes accessed | tf_op | source)
XLA Modules:
  0.0 98.9 jit_solution(2118064087796770987)
XLA Ops:
  0.6 94.1 %prefill.1 = (bf16[1024,512]{1,0:T(8,128)(2,1)}, bf16[4,256,256]{2,1,0:T(8,128)(2,1)}) custom-call(s32[64]{0:T(128)} %bitcast.17, s32[64]{0:T(128)} %hs_ref.1, s32[16,64]{1,0:T(8,128)} %bitcast.14, s32[16,64]{1,0:T(8,128)} %bitcast.15, s32[64]{0:T(128)} %pre_ref.1, s32[64]{0:T(128)} %suf_ref.1, f32[8]{0:T(128)} %decay_ref.1, f32[8]{0:T(128)} %skip_ref.1, ...), custom_call_target="tpu_custom_call" | custom-call | flops 5000000000 | bytes 16777216 | tf_op jit(solution)/shard_map/prefill/pallas_call | solution.py:461
  94.8 2.3 %copy.20 = bf16[1024,512]{1,0:T(8,128)(2,1)} copy(bf16[1024,512]{1,0:T(8,128)(2,1)} %get-tuple-element.8) | data formatting | bytes 2097152
  97.0 1.9 %copy.21 = bf16[1024,256]{1,0:T(8,128)(2,1)} copy(bf16[1024,256]{1,0:T(8,128)(2,1)} %bitcast.10) | data formatting | bytes 1048576
